TPU v7x, 128 devices: a whole 4x4x4 slice. The times are simulated.
128 devices in a mesh: facet: 8 (over z, core), vis: 16 (over y, x).
Axes of the slice: x: 4, y: 4, z: 4, core: 2. Of those that a mesh axis runs over, the one named last changes fastest.
Arguments:
- model: bfloat16 [2048, 2048], P(('facet', 'vis')), may hold values from -0.005859375 to 0.005859375
- observed: bfloat16 [1024, 2, 128, 128], P(('facet', 'vis')), may hold values from -6 to 6
- u_offsets: int32 [1024], P(('facet', 'vis')), may hold values from 0 to 32767
- v_offsets: int32 [1024], P(('facet', 'vis')), may hold values from 0 to 32767
- facet_lists: int32 [1024, 2], P(('facet', 'vis')), may hold values from 0 to 7, all different within a row; in each aligned block of 8 rows (0 to 7, 8 to 15, ...) at most 2 rows name the same one
Outputs:
- dirty: float32 [2048, 2048], P(('facet', 'vis'))
- residual: bfloat16 [1024, 2, 128, 128], P(('facet', 'vis'))
Inputs may be any that keep to these rules, and one draw needn't show every extreme that they name: `facet_lists`: each row names 2 different facets; among the 8 subgrids of one device no facet is named more than 2 times, and that many is reached.
All inputs are finite; a program needn't handle non-finite values.
Results may differ from a plain program's by a relative error of at most 0.018.
Values may be sent and summed in bfloat16 or wider, within the bound.
A program may use at most 128 MiB of HBM per device.

v0:
```python
import jax
import jax.numpy as jnp
from jax import lax
from jax.sharding import PartitionSpec as P

IMG = 32768


two_pi = 6.283185307179586


def phase_table(offsets, length, coords, period):
    steps = offsets[..., None] + jnp.arange(length, dtype=jnp.int32)
    index = steps[..., :, None] * coords[..., None, :] % period
    angle = index.astype(jnp.float32) * jnp.float32(two_pi / period)
    return (jnp.cos(angle).astype(jnp.bfloat16), jnp.sin(angle).astype(jnp.bfloat16))


def body(model, observed, u_offsets, v_offsets, facet_lists):
    groups = observed.shape[0]
    side = observed.shape[2]
    fr_dev = model.shape[0]
    width = model.shape[1]
    listed = facet_lists.shape[1]
    facet_count = lax.axis_size("facet")
    n_vis = lax.axis_size("vis")
    facet_rows = fr_dev * n_vis
    facet_step = IMG // facet_count
    local = jnp.arange(facet_rows, dtype=jnp.int32)
    column_count = jnp.arange(width, dtype=jnp.int32)
    own_coords = lax.axis_index("facet") * facet_step + local
    slot_capacity = max(2, (groups * listed + facet_count - 1) // facet_count)
    facet_ids = jnp.arange(facet_count, dtype=jnp.int32)
    hit = jnp.any(facet_lists[:, :, None] == facet_ids[None, None, :], axis=1).astype(jnp.int32)
    position = jnp.cumsum(hit, axis=0) - hit
    slot_ids = jnp.arange(slot_capacity, dtype=jnp.int32)
    selection_mask = (hit[:, :, None] == 1) & (position[:, :, None] == slot_ids[None, None, :])
    offsets = jnp.stack([u_offsets, v_offsets], axis=1)
    packed_offsets = jnp.sum(
        selection_mask.astype(jnp.int32)[:, :, :, None] * offsets[:, None, None, :], axis=0
    )
    cos_v, sin_v = phase_table(v_offsets, side, column_count, IMG)
    whole = lax.all_gather(model, ("facet", "vis"), axis=0, tiled=True)
    chosen = whole.reshape(facet_count, facet_rows, width)[facet_lists]
    coords = facet_lists[:, :, None] * facet_step + local[None, None, :]
    u_pairs = jnp.broadcast_to(u_offsets[:, None], (groups, listed))
    cos_u, sin_u = phase_table(u_pairs, side, coords, IMG)
    w_real = jnp.einsum(
        "gkax,gkxy->gkay", cos_u, chosen, preferred_element_type=jnp.float32
    ).astype(jnp.bfloat16)
    w_imag = (
        -jnp.einsum("gkax,gkxy->gkay", sin_u, chosen, preferred_element_type=jnp.float32)
    ).astype(jnp.bfloat16)
    p_real = jnp.einsum(
        "gkay,gby->gab", w_real, cos_v, preferred_element_type=jnp.float32
    ) + jnp.einsum("gkay,gby->gab", w_imag, sin_v, preferred_element_type=jnp.float32)
    predicted_imaginary = jnp.einsum(
        "gkay,gby->gab", w_imag, cos_v, preferred_element_type=jnp.float32
    ) - jnp.einsum("gkay,gby->gab", w_real, sin_v, preferred_element_type=jnp.float32)
    res_real = (observed[:, 0].astype(jnp.float32) - p_real).astype(jnp.bfloat16)
    res_imag = (observed[:, 1].astype(jnp.float32) - predicted_imaginary).astype(jnp.bfloat16)
    residual = jnp.stack([res_real, res_imag], axis=1)
    packed = jnp.einsum(
        "exi,emtz->ximtz",
        selection_mask.astype(jnp.bfloat16),
        residual,
        preferred_element_type=jnp.float32,
    ).astype(jnp.bfloat16)
    arrived = lax.all_to_all(packed, "facet", split_axis=0, concat_axis=0, tiled=True)
    arrived_offsets = lax.all_to_all(
        packed_offsets, "facet", split_axis=0, concat_axis=0, tiled=True
    )
    item_offsets = arrived_offsets.reshape(facet_count * slot_capacity, 2)
    cos_r, sin_r = phase_table(item_offsets[:, 0], side, own_coords, IMG)
    item_cos_c, item_sin_c = phase_table(item_offsets[:, 1], side, column_count, IMG)
    cos_r, sin_r, cos_c, sin_c = (cos_r, sin_r, item_cos_c, item_sin_c)
    items = arrived.reshape(facet_count * slot_capacity, 2, side, side)
    row_real = (
        jnp.einsum("nax,nab->nxb", cos_r, items[:, 0], preferred_element_type=jnp.float32)
        - jnp.einsum("nax,nab->nxb", sin_r, items[:, 1], preferred_element_type=jnp.float32)
    ).astype(jnp.bfloat16)
    row_imag = (
        jnp.einsum("nax,nab->nxb", cos_r, items[:, 1], preferred_element_type=jnp.float32)
        + jnp.einsum("nax,nab->nxb", sin_r, items[:, 0], preferred_element_type=jnp.float32)
    ).astype(jnp.bfloat16)
    summed = lax.psum_scatter(
        (
            jnp.einsum("nxb,nby->xy", row_real, cos_c, preferred_element_type=jnp.float32)
            - jnp.einsum("nxb,nby->xy", row_imag, sin_c, preferred_element_type=jnp.float32)
        ).astype(jnp.bfloat16),
        "vis",
        scatter_dimension=0,
        tiled=True,
    ).astype(jnp.float32)
    dirty = summed * (1.0 / (side * side))
    return (dirty, residual)


def solution(mesh):
    in_specs = (
        P(("facet", "vis"), None),
        P(("facet", "vis"), None, None, None),
        P(("facet", "vis")),
        P(("facet", "vis")),
        P(("facet", "vis"), None),
    )
    out_specs = (P(("facet", "vis"), None), P(("facet", "vis"), None, None, None))
    return jax.shard_map(body, mesh=mesh, in_specs=in_specs, out_specs=out_specs, check_vma=False)
```

profile of v0, /device:TPU:0, one launch (start us, length us, event | category | flops | bytes accessed | tf_op | source)
XLA Modules:
  0.0 469.4 jit_solution(14993752717213735335)
XLA Ops:
  7.9 0.8 fusion.44
  9.7 0.7 copy.42
  10.4 5.4 %all-to-all-start = ((s32[8,2,2]{1,2,0:T(2,128)}), s32[8,2,2]{1,2,0:T(2,128)S(1)}, u32[]{:S(2)}, u32[]{:S(2)}) async-start(s32[8,2,2]{1,2,0:T(2,128)} %copy.42), calls=%async_computation | async-start | bytes 16384 | tf_op jit(solution)/shard_map/all_to_all | solution.py:70
  16.7 0.7 iota_add_fusion.4
  17.5 0.7 iota_add_fusion.2
  18.3 32.6 %cosine_convert_fusion.22 = bf16[8,128,2048]{2,1,0:T(8,128)(2,1)} fusion(s32[8,128]{1,0:T(8,128)S(1)} %iota_add_fusion.4), kind=kLoop, calls=%fused_computation.24.clone.1.clone | loop fusion | flops 31457280 | bytes 4198400 | tf_op jit(solution)/shard_map/gkay,gby->gab/dot_general | solution.py:54
  50.8 32.7 %sine_convert_fusion.45 = bf16[8,128,2048]{2,1,0:T(8,128)(2,1)} fusion(s32[8,128]{1,0:T(8,128)S(1)} %iota_add_fusion.4), kind=kLoop, calls=%fused_computation.23.clone.1.clone.clone.clone.clone.clone.clone.clone.clone.clo... | loop fusion | flops 31457280 | bytes 4198400 | tf_op jit(solution)/shard_map/gkay,gby->gab/dot_general | solution.py:56
  83.5 32.5 %cosine_convert_fusion.21 = bf16[8,128,2048]{2,1,0:T(8,128)(2,1)} fusion(s32[8,128]{1,0:T(8,128)S(1)} %iota_add_fusion.4), kind=kLoop, calls=%fused_computation.24.clone.clone.1 | loop fusion | flops 31457280 | bytes 4198400 | tf_op jit(solution)/shard_map/gkay,gby->gab/dot_general | solution.py:57
  116.0 32.7 %sine_convert_fusion.46 = bf16[8,128,2048]{2,1,0:T(8,128)(2,1)} fusion(s32[8,128]{1,0:T(8,128)S(1)} %iota_add_fusion.4), kind=kLoop, calls=%fused_computation.23.clone.clone.clone.clone.clone.clone.clone.clone.clone.clone.1 | loop fusion | flops 31457280 | bytes 4198400 | tf_op jit(solution)/shard_map/gkay,gby->gab/dot_general | solution.py:59
  148.7 10.6 %gather_fusion = bf16[16,256,2048]{2,1,0:T(8,128)(2,1)} fusion(bf16[8,256,2048]{2,1,0:T(8,128)(2,1)} %bitcast.86, s32[1024]{0:T(1024)S(1)} %pad_clamp_fusion), kind=kCustom, calls=%fused_computation | custom fusion | bytes 33554496 | tf_op jit(solution)/shard_map/gather | solution.py:44
  159.3 14.7 %convert_reduce_fusion.1 = bf16[8,128,2048]{2,1,0:T(8,128)(2,1)S(1)} fusion(bf16[8,2,256,2048]{3,2,1,0:T(8,128)(2,1)} %bitcast.87, s32[8,2,256]{2,1,0:T(2,128)S(1)} %iota_add_fusion, s32[8,2,128]{2,1,0:T(2,128)S(1)} %iota_add_fusion.2), kind=kOutput, calls=%fused_computation.13 | convolution fusion | flops 2165833728 | bytes 20996096 | tf_op jit(solution)/shard_map/gkax,gkxy->gkay/dot_general | solution.py:48
  174.0 15.6 %convert_reduce_fusion = bf16[8,128,2048]{2,1,0:T(8,128)(2,1)S(1)} fusion(bf16[8,2,256,2048]{3,2,1,0:T(8,128)(2,1)} %bitcast.88, s32[8,2,256]{2,1,0:T(2,128)S(1)} %iota_add_fusion, s32[8,2,128]{2,1,0:T(2,128)S(1)} %iota_add_fusion.2), kind=kOutput, calls=%fused_computation.11 | convolution fusion | flops 2170028032 | bytes 20996096 | tf_op jit(solution)/shard_map/gkax,gkxy->gkay/dot_general | solution.py:52
  189.6 1.2 fusion.17
  190.9 0.9 copy-done.3
  191.8 1.2 fusion.16
  193.1 0.9 copy-done.1
  194.1 1.3 fusion.36
  195.4 0.9 copy-done
  196.3 1.3 fusion.37
  198.1 1.2 copy.49
  199.3 4.8 %all-to-all-start.1 = ((bf16[8,2,2,128,128]{4,3,2,1,0:T(8,128)(2,1)}), bf16[8,2,2,128,128]{4,3,2,1,0:T(8,128)(2,1)S(1)}, u32[]{:S(2)}, u32[]{:S(2)}) async-start(bf16[8,2,2,128,128]{4,3,2,1,0:T(8,128)(2,1)} %copy.49), calls=%async_computation.1 | async-start | bytes 2097152 | tf_op jit(solution)/shard_map/all_to_all | solution.py:69
  204.1 8.8 %reduce-scatter.2.cloned.1.call-start = ((), (), s32[]{:S(2)}) async-start(), calls=%async_computation.4 | async-start | bytes 1114112 | tf_op jit(solution)/shard_map/reduce_scatter | solution.py:86
  213.1 7.0 %all-to-all-done.1 = bf16[8,2,2,128,128]{4,3,2,1,0:T(8,128)(2,1)S(1)} async-done(((bf16[8,2,2,128,128]{4,3,2,1,0:T(8,128)(2,1)}), bf16[8,2,2,128,128]{4,3,2,1,0:T(8,128)(2,1)S(1)}, u32[]{:S(2)}, u32[]{:S(2)}) %all-to-all-start.1) | async-done | bytes 1048608 | tf_op jit(solution)/shard_map/all_to_all | solution.py:69
  220.1 7.8 %fusion.41 = f32[16,256,128]{2,1,0:T(8,128)S(1)} fusion(s32[256]{0:T(256)S(1)} %iota_add_fusion.5, s32[16,128]{1,0:T(8,128)S(1)} %get-tuple-element.17, bf16[16,2,128,128]{3,2,1,0:T(8,128)(2,1)S(1)} %bitcast.89), kind=kOutput, calls=%fused_computation.68 | convolution fusion | flops 142082048 | bytes 2630656 | tf_op jit(solution)/shard_map/nax,nab->nxb/dot_general | solution.py:79
  227.9 8.0 %fusion.40 = f32[16,256,128]{2,1,0:T(8,128)S(1)} fusion(s32[256]{0:T(256)S(1)} %iota_add_fusion.5, s32[16,128]{1,0:T(8,128)S(1)} %get-tuple-element.17, bf16[16,2,128,128]{3,2,1,0:T(8,128)(2,1)S(1)} %bitcast.90), kind=kOutput, calls=%fused_computation.67 | convolution fusion | flops 142082048 | bytes 2630656 | tf_op jit(solution)/shard_map/nax,nab->nxb/dot_general | solution.py:83
  235.8 8.1 %subtract_convert_fusion.clone.5 = bf16[16,256,128]{2,1,0:T(8,128)(2,1)S(1)} fusion(f32[16,256,128]{2,1,0:T(8,128)S(1)} %fusion.41, s32[256]{0:T(256)S(1)} %iota_add_fusion.5, s32[16,128]{1,0:T(8,128)S(1)} %get-tuple-element.17, bf16[16,2,128,128]{3,2,1,0:T(8,128)(2,1)S(1)} %bitcast.91), kind=kOutput, calls=%fused_computation.53.clone.clone.clone.2 | convolution fusion | flops 143130624 | bytes 3679232 | tf_op jit(solution)/shard_map/nax,nab->nxb/dot_general | solution.py:80
  243.9 8.1 %add_convert_fusion.clone.5 = bf16[16,256,128]{2,1,0:T(8,128)(2,1)S(1)} fusion(f32[16,256,128]{2,1,0:T(8,128)S(1)} %fusion.40, s32[256]{0:T(256)S(1)} %iota_add_fusion.5, s32[16,128]{1,0:T(8,128)S(1)} %get-tuple-element.17, bf16[16,2,128,128]{3,2,1,0:T(8,128)(2,1)S(1)} %bitcast.92), kind=kOutput, calls=%fused_computation.52.clone.clone.clone.2 | convolution fusion | flops 143130624 | bytes 3679232 | tf_op jit(solution)/shard_map/nax,nab->nxb/dot_general | solution.py:84
  252.0 67.9 %fusion.20 = f32[256,2048]{1,0:T(8,128)S(1)} fusion(s32[16,128]{1,0:T(8,128)S(1)} %get-tuple-element.16, bf16[16,256,128]{2,1,0:T(8,128)(2,1)S(1)} %add_convert_fusion.clone.5), kind=kOutput, calls=%fused_computation.42 | convolution fusion | flops 2210398208 | bytes 3153920 | tf_op jit(solution)/shard_map/nxb,nby->xy/dot_general | solution.py:89
  319.9 68.1 %fusion.23 = bf16[256,2048]{1,0:T(8,128)(2,1)} fusion(f32[256,2048]{1,0:T(8,128)S(1)} %fusion.20, s32[16,128]{1,0:T(8,128)S(1)} %get-tuple-element.16, bf16[16,256,128]{2,1,0:T(8,128)(2,1)S(1)} %subtract_convert_fusion.clone.5), kind=kOutput, calls=%fused_computation.45 | convolution fusion | flops 2211446784 | bytes 4202496 | tf_op jit(solution)/shard_map/nxb,nby->xy/dot_general | solution.py:88
  388.1 0.8 copy.52
  388.9 71.7 %reduce-scatter.2.cloned.1.call-done = bf16[16,2048]{1,0:T(8,128)(2,1)} async-done(((bf16[256,2048]{1,0:T(8,128)(2,1)}), bf16[16,2048]{1,0:T(8,128)(2,1)}) %reduce-scatter.2.cloned.1.call-update) | async-done | bytes 65552 | tf_op jit(solution)/shard_map/reduce_scatter | solution.py:86
  460.6 1.5 convert_multiply_fusion
  (34 shorter events, 3.6 us)
Async XLA Ops:
  7.2 141.5 %all-gather.2.cloned.1.call-start = ((), (), s32[]{:S(2)}) async-start(), calls=%async_computation.3 | async-start | bytes 8454144 | tf_op jit(solution)/shard_map/all_gather | solution.py:43
  10.4 188.9 %all-to-all-start = ((s32[8,2,2]{1,2,0:T(2,128)}), s32[8,2,2]{1,2,0:T(2,128)S(1)}, u32[]{:S(2)}, u32[]{:S(2)}) async-start(s32[8,2,2]{1,2,0:T(2,128)} %copy.42), calls=%async_computation | async-start | bytes 16384 | tf_op jit(solution)/shard_map/all_to_all | solution.py:70
  174.0 15.6 %copy-start.2 = (bf16[8,128,2048]{2,1,0:T(8,128)(2,1)S(1)}, bf16[8,128,2048]{2,1,0:T(8,128)(2,1)}, u32[]{:S(2)}) copy-start(bf16[8,128,2048]{2,1,0:T(8,128)(2,1)} %cosine_convert_fusion.22) | copy-start | bytes 12582916
  189.6 2.2 copy-start.3
  191.8 2.2 copy-start.1
  191.8 2.3 copy-start.4
  194.1 2.2 copy-start
  199.3 20.8 %all-to-all-start.1 = ((bf16[8,2,2,128,128]{4,3,2,1,0:T(8,128)(2,1)}), bf16[8,2,2,128,128]{4,3,2,1,0:T(8,128)(2,1)S(1)}, u32[]{:S(2)}, u32[]{:S(2)}) async-start(bf16[8,2,2,128,128]{4,3,2,1,0:T(8,128)(2,1)} %copy.49), calls=%async_computation.1 | async-start | bytes 2097152 | tf_op jit(solution)/shard_map/all_to_all | solution.py:69
  204.1 256.5 %reduce-scatter.2.cloned.1.call-start = ((), (), s32[]{:S(2)}) async-start(), calls=%async_computation.4 | async-start | bytes 1114112 | tf_op jit(solution)/shard_map/reduce_scatter | solution.py:86
Sparse Core Ops, SparseCore 0:
  11.1 73.1 all-gather.1
  388.2 72.4 reduce-scatter.1
where the time goes:
time: 477 us; the launch traced here: 469 us
  matrix products  204 us (43%)
  other arithmetic  136 us (29%)
  waiting for transfers between devices  79.4 us (17%)
  starting transfers between devices  19 us (4%)
  local copies, waits for them, and re-layouts  16.8 us (4%)
  between operations  14.6 us (3%)
    reduce_scatter x1, waiting for transfers between devices, body(): lax.psum_scatter((jnp.einsum('nxb,nby->xy', row_real, cos_c, preferred_el...  71.7 us
    dot_general x1, matrix products, body(): jnp.einsum('nxb,nby->xy', row_real, cos_c, preferred_element_type=jnp.flo...  68.1 us
    dot_general x1, matrix products, body(): jnp.einsum('nxb,nby->xy', row_imag, sin_c, preferred_element_type=jnp.flo...  67.9 us
    dot_general x1, other arithmetic, body(): jnp.einsum('gkay,gby->gab', w_imag, sin_v, preferred_element_type=jnp.flo...  32.7 us
    dot_general x1, other arithmetic, body(): jnp.einsum('gkay,gby->gab', w_real, sin_v, preferred_element_type=jnp.flo...  32.7 us
    dot_general x1, other arithmetic, body(): jnp.einsum('gkay,gby->gab', w_real, cos_v, preferred_element_type=jnp.flo...  32.6 us
    dot_general x1, other arithmetic, body(): jnp.einsum('gkay,gby->gab', w_imag, cos_v, preferred_element_type=jnp.flo...  32.5 us
    dot_general x1, matrix products, body(): jnp.einsum('gkax,gkxy->gkay', sin_u, chosen, preferred_element_type=jnp.f...  15.6 us
  transfers between devices with their start and end apart: 4, of which 2 were waited for; matrix products, arithmetic and copies ran while one was open for 39% of the time, Pallas kernels for 0%

commit v1 on v0

v1 whole, which is shorter than its diff:
```python
import math

import jax
import jax.numpy as jnp
from jax import lax
from jax.experimental import pallas as pl
from jax.experimental.pallas import tpu as pltpu
from jax.sharding import PartitionSpec as P

IMG = 32768
LANES = 128
NF = 8
NV = 16
S = 128
FW = 2048
FRT = 256
ROWS = 16
G = 8
YC = FW // LANES
XC = FRT // LANES
STEP = IMG // NF
MESH = pl.DeviceIdType.MESH
F32 = jnp.float32
BF16 = jnp.bfloat16
NT = (((1,), (1,)), ((), ()))
NN = (((1,), (0,)), ((), ()))


def sincos(index):
    quarter = (index + IMG // 8) >> 13
    rest = index - (quarter << 13)
    angle = rest.astype(F32) * F32(2.0 * math.pi / IMG)
    t = angle * angle
    sn = angle * (1.0 + t * (-1.0 / 6 + t * (1.0 / 120 + t * (-1.0 / 5040 + t * (1.0 / 362880)))))
    cs = 1.0 + t * (-0.5 + t * (1.0 / 24 + t * (-1.0 / 720 + t * (1.0 / 40320))))
    odd = (quarter & 1) == 1
    c = jnp.where(odd, sn, cs)
    s = jnp.where(odd, cs, sn)
    c = jnp.where(((quarter + 1) & 2) != 0, -c, c)
    s = jnp.where((quarter & 2) != 0, -s, s)
    return c, s


def iota(shape, axis):
    return lax.broadcasted_iota(jnp.int32, shape, axis)


def kernel(
    model, observed, u_off, v_off, lists, dirty, residual,
    image, uv_out, uv_in, e_c, e_s, g_c, g_s, pv_c, pv_s, pu_c, pu_s, cv, cu, cut,
    p_out, p_in, r_out, r_in, total, d_out, d_in,
    ag_ss, ag_rs, uv_ss, uv_rs, p_ss, p_rs, r_ss, r_rs, d_ss, d_rs,
):
    f = lax.axis_index("facet")
    j = lax.axis_index("vis")

    def other_facet(h):
        return {"facet": h, "vis": j}

    def other_vis(k):
        return {"facet": f, "vis": k}

    barrier = pltpu.get_barrier_semaphore()
    for d in range(1, NV):
        pl.semaphore_signal(barrier, inc=1, device_id=other_vis(lax.rem(j + d, NV)), device_id_type=MESH)
    for d in range(1, NF):
        pl.semaphore_signal(barrier, inc=1, device_id=other_facet(lax.rem(f + d, NF)), device_id_type=MESH)
    pl.semaphore_wait(barrier, NV - 1 + NF - 1)

    def remote(src, dst, ss, rs, device):
        return pltpu.make_async_remote_copy(
            src_ref=src, dst_ref=dst, send_sem=ss, recv_sem=rs, device_id=device, device_id_type=MESH
        )

    def ag_copy(sender, target):
        return remote(
            model, image.at[pl.ds(pl.multiple_of(sender * ROWS, ROWS), ROWS), :],
            ag_ss.at[target], ag_rs.at[sender], other_vis(target),
        )

    first, last = [], []
    hits = [[lists[g, k] for k in range(2)] for g in range(G)]
    for h in range(NF):
        lo, hi = jnp.int32(0), jnp.int32(0)
        for g in range(G):
            named = (hits[g][0] == h) | (hits[g][1] == h)
            hi = jnp.where(named, g, hi)
        for g in reversed(range(G)):
            named = (hits[g][0] == h) | (hits[g][1] == h)
            lo = jnp.where(named, g, lo)
        first.append(lo)
        last.append(hi)

    row = iota((8, LANES), 0)
    for h in range(NF):
        a, b = first[h], last[h]
        uv_out[h] = jnp.where(
            row == 0, u_off[a], jnp.where(row == 1, u_off[b], jnp.where(row == 2, v_off[a], v_off[b]))
        )

    def uv_copy(sender, target):
        return remote(uv_out.at[target], uv_in.at[sender], uv_ss.at[target], uv_rs.at[sender], other_facet(target))

    def far_first(i):
        q = i // 2
        dz = jnp.where(q == 0, 2, jnp.where(q == 1, 1, jnp.where(q == 2, 3, 0)))
        z = lax.rem(f // 2 + dz, 4)
        c = lax.rem(lax.rem(f, 2) + 1 + lax.rem(i, 2), 2)
        return z * 2 + c

    @pl.loop(0, NF - 1)
    def _(i):
        uv_copy(f, far_first(i)).start()

    @pl.loop(1, NV)
    def _(d):
        ag_copy(j, lax.rem(j + d, NV)).start()

    image[pl.ds(pl.multiple_of(j * ROWS, ROWS), ROWS), :] = model[...]
    uv_in[f] = uv_out[f]

    lane = iota((S, LANES), 1)
    sub = iota((S, LANES), 0)

    @pl.loop(0, YC)
    def _(r):
        c, s = sincos((sub * (r * LANES + lane)) & (IMG - 1))
        e_c[r] = c
        e_s[r] = s

    @pl.loop(0, XC)
    def _(r):
        c, s = sincos((sub * (f * STEP + r * LANES + lane)) & (IMG - 1))
        g_c[r] = c
        g_s[r] = s

    @pl.loop(0, NF - 1)
    def _(i):
        uv_copy(far_first(i), far_first(i)).wait_recv()

    y_of = iota((YC, LANES), 0) * LANES + iota((YC, LANES), 1)
    x_of = iota((8, LANES), 0) * LANES + iota((8, LANES), 1) + f * STEP

    @pl.loop(0, NF)
    def _(h):
        for s in range(2):
            u = uv_in[h, s : s + 1, :]
            v = uv_in[h, 2 + s : 3 + s, :]
            c, sn = sincos((v * y_of) & (IMG - 1))
            pv_c[2 * h + s] = c
            pv_s[2 * h + s] = sn
            c, sn = sincos((u * x_of) & (IMG - 1))
            pu_c[2 * h + s] = c
            pu_s[2 * h + s] = sn

    @pl.loop(0, 2 * NF)
    def _(n):
        @pl.loop(0, YC)
        def _(r):
            pc = pv_c[n, pl.ds(r, 1), :]
            ps = pv_s[n, pl.ds(r, 1), :]
            ec, es = e_c[r], e_s[r]
            at = pl.ds(pl.multiple_of(r * LANES, LANES), LANES)
            cv[n, 0:S, at] = (pc * ec - ps * es).astype(BF16)
            cv[n, S : 2 * S, at] = (ps * ec + pc * es).astype(BF16)

        for r in range(XC):
            pc = pu_c[n, r : r + 1, :]
            ps = pu_s[n, r : r + 1, :]
            ec, es = g_c[r], g_s[r]
            at = slice(r * LANES, (r + 1) * LANES)
            c = pc * ec - ps * es
            s = ps * ec + pc * es
            cu[n, 0:S, at] = c.astype(BF16)
            cu[n, S : 2 * S, at] = s.astype(BF16)
            cut[n, at, 0:S] = c.T.astype(BF16)
            cut[n, at, S : 2 * S] = s.T.astype(BF16)

    @pl.loop(1, NV)
    def _(d):
        k = lax.rem(j + d, NV)
        ag_copy(k, k).wait_recv()

    def predict(h):
        for s in range(2):
            n = 2 * h + s
            t = lax.dot_general(cv[n], image[...], NT, preferred_element_type=F32).astype(BF16)
            o = lax.dot_general(cu[n], t, NT, preferred_element_type=F32)
            yield s, (o[0:S, 0:S] - o[S:, S:]).astype(BF16), (-(o[S:, 0:S] + o[0:S, S:])).astype(BF16)

    def p_copy(sender, target):
        return remote(
            p_out.at[target], p_in.at[pl.ds(2 * sender, 2)], p_ss.at[target], p_rs.at[sender], other_facet(target)
        )

    @pl.loop(0, NF)
    def _(i):
        h = far_first(i)
        for s, re, im in predict(h):
            p_out[h, s, 0] = re
            p_out[h, s, 1] = im

        @pl.when(i < NF - 1)
        def _():
            p_copy(f, h).start()

    for s in range(2):
        p_in[2 * f + s] = p_out[f, s]

    @pl.loop(0, NF - 1)
    def _(i):
        p_copy(far_first(i), far_first(i)).wait_recv()

    for g in range(G):
        acc = observed[g].astype(F32)
        for k in range(2):
            h = hits[g][k]
            slot = jnp.int32(0)
            for e in range(g):
                slot = jnp.where((hits[e][0] == h) | (hits[e][1] == h), 1, slot)
            acc = acc - p_in[2 * h + slot].astype(F32)
        residual[g] = acc.astype(BF16)

    def r_copy(sender, target):
        return remote(
            r_out.at[pl.ds(2 * target, 2)], r_in.at[pl.ds(2 * sender, 2)],
            r_ss.at[target], r_rs.at[sender], other_facet(target),
        )

    for h in range(NF):
        r_out[2 * h] = residual[first[h]]
        r_out[2 * h + 1] = residual[last[h]]

    @pl.loop(0, NF - 1)
    def _(i):
        r_copy(f, far_first(i)).start()

    for s in range(2):
        r_in[2 * f + s] = r_out[2 * f + s]

    total[...] = jnp.zeros_like(total)

    @pl.loop(0, NF)
    def _(i):
        h = far_first(NF - 1 - i)

        @pl.when(i > 0)
        def _():
            r_copy(h, h).wait_recv()

        for s in range(2):
            n = 2 * h + s
            re = r_in[n, 0]
            im = r_in[n, 1]
            top = jnp.concatenate([re, -im], axis=1)
            bottom = jnp.concatenate([-im, -re], axis=1)
            both = jnp.concatenate([top, bottom], axis=0)
            z = lax.dot_general(cut[n], both, NN, preferred_element_type=F32).astype(BF16)
            total[...] += lax.dot_general(z, cv[n], NN, preferred_element_type=F32)

    def d_copy(sender, target):
        return remote(d_out.at[target], d_in.at[sender], d_ss.at[target], d_rs.at[sender], other_vis(target))

    @pl.loop(0, NV)
    def _(k):
        d_out[k] = total[pl.ds(pl.multiple_of(k * ROWS, ROWS), ROWS), :].astype(BF16)

    @pl.loop(1, NV)
    def _(d):
        d_copy(j, lax.rem(j + d, NV)).start()

    acc = total[pl.ds(pl.multiple_of(j * ROWS, ROWS), ROWS), :]
    dirty[...] = acc

    @pl.loop(1, NV)
    def _(d):
        k = lax.rem(j + d, NV)
        d_copy(k, k).wait_recv()
        dirty[...] += d_in[k].astype(F32)

    dirty[...] = dirty[...] * F32(1.0 / (S * S))

    @pl.loop(0, NF - 1)
    def _(i):
        h = far_first(i)
        uv_copy(f, h).wait_send()
        p_copy(f, h).wait_send()
        r_copy(f, h).wait_send()

    @pl.loop(1, NV)
    def _(d):
        k = lax.rem(j + d, NV)
        ag_copy(j, k).wait_send()
        d_copy(j, k).wait_send()


def body(model, observed, u_offsets, v_offsets, facet_lists):
    vm = pl.BlockSpec(memory_space=pltpu.VMEM)
    sm = pl.BlockSpec(memory_space=pltpu.SMEM)
    dma = pltpu.SemaphoreType.DMA
    return tuple(
        pl.pallas_call(
            kernel,
            name="major_cycle",
            out_shape=(
                jax.ShapeDtypeStruct((ROWS, FW), F32),
                jax.ShapeDtypeStruct((G, 2, S, S), BF16),
            ),
            in_specs=[vm, vm, sm, sm, sm],
            out_specs=(vm, vm),
            scratch_shapes=[
                pltpu.VMEM((FRT, FW), BF16),
                pltpu.VMEM((NF, 8, LANES), jnp.int32),
                pltpu.VMEM((NF, 8, LANES), jnp.int32),
                pltpu.VMEM((YC, S, LANES), F32),
                pltpu.VMEM((YC, S, LANES), F32),
                pltpu.VMEM((XC, S, LANES), F32),
                pltpu.VMEM((XC, S, LANES), F32),
                pltpu.VMEM((2 * NF, YC, LANES), F32),
                pltpu.VMEM((2 * NF, YC, LANES), F32),
                pltpu.VMEM((2 * NF, 8, LANES), F32),
                pltpu.VMEM((2 * NF, 8, LANES), F32),
                pltpu.VMEM((2 * NF, 2 * S, FW), BF16),
                pltpu.VMEM((2 * NF, 2 * S, FRT), BF16),
                pltpu.VMEM((2 * NF, FRT, 2 * S), BF16),
                pltpu.VMEM((NF, 2, 2, S, S), BF16),
                pltpu.VMEM((2 * NF, 2, S, S), BF16),
                pltpu.VMEM((2 * NF, 2, S, S), BF16),
                pltpu.VMEM((2 * NF, 2, S, S), BF16),
                pltpu.VMEM((FRT, FW), F32),
                pltpu.VMEM((NV, ROWS, FW), BF16),
                pltpu.VMEM((NV, ROWS, FW), BF16),
                dma((NV,)), dma((NV,)), dma((NF,)), dma((NF,)), dma((NF,)), dma((NF,)),
                dma((NF,)), dma((NF,)), dma((NV,)), dma((NV,)),
            ],
            compiler_params=pltpu.CompilerParams(
                collective_id=0, has_side_effects=True, vmem_limit_bytes=56 << 20
            ),
        )(model, observed, u_offsets, v_offsets, facet_lists)
    )


def solution(mesh):
    in_specs = (
        P(("facet", "vis"), None),
        P(("facet", "vis"), None, None, None),
        P(("facet", "vis")),
        P(("facet", "vis")),
        P(("facet", "vis"), None),
    )
    out_specs = (P(("facet", "vis"), None), P(("facet", "vis"), None, None, None))
    return jax.shard_map(body, mesh=mesh, in_specs=in_specs, out_specs=out_specs, check_vma=False)
```

time: 477 us -> 81 us (0.17); the launches traced: 469 us -> 80 us
  matrix products: 204 us -> 0 us
  other arithmetic: 136 us -> 0 us
  waiting for transfers between devices: 79.4 us -> 0 us
  Pallas kernels: 0 us -> 74.6 us
  starting transfers between devices: 19 us -> 0 us
  between operations: 14.6 us -> 0.64 us
  local copies, waits for them, and re-layouts: 16.8 us -> 4.8 us
    dot_general x13 -> x0, matrix products: 204 us -> none  [the longest x1 68.1 us: body(): jnp.einsum('nxb,nby->xy', row_real, cos_c, preferred_element_type=jnp.flo...]
    dot_general x4 -> x0, other arithmetic: 130 us -> none  [the longest x1 32.7 us: body(): jnp.einsum('gkay,gby->gab', w_imag, sin_v, preferred_element_type=jnp.flo...]
    pallas_call x0 -> x1, Pallas kernels: none -> 74.6 us  [body(): pl.pallas_call(kernel, name='major_cycle', out_shape=(jax.ShapeDtypeStruc...]
    reduce_scatter x1 -> x0, waiting for transfers between devices: 71.7 us -> none  [body(): lax.psum_scatter((jnp.einsum('nxb,nby->xy', row_real, cos_c, preferred_el...]
    gather x1 -> x0, local copies, waits for them, and re-layouts: 10.6 us -> none  [body(): chosen = whole.reshape(facet_count, facet_rows, width)[facet_lists]]
    all_to_all x2 -> x0, starting transfers between devices: 10.2 us -> none  [the longest x1 5.4 us: body(): lax.all_to_all(packed_offsets, 'facet', split_axis=0, concat_axis=0, tile...]
    reduce_scatter x1 -> x0, starting transfers between devices: 8.78 us -> none  [body(): lax.psum_scatter((jnp.einsum('nxb,nby->xy', row_real, cos_c, preferred_el...]
    all_to_all x2 -> x0, waiting for transfers between devices: 6.99 us -> none  [the longest x1 6.99 us: body(): lax.all_to_all(packed, 'facet', split_axis=0, concat_axis=0, tiled=True)]
  transfers between devices with their start and end apart: 4 -> 0, of which waited for: 2 -> 0; matrix products, arithmetic and copies ran while one was open for 39% -> 0% of each run, Pallas kernels for 0% -> 0%
where the time goes in v1:
time: 81 us; the launch traced here: 80 us
  Pallas kernels  74.6 us (92%)
  local copies, waits for them, and re-layouts  4.8 us (6%)
    pallas_call x1, Pallas kernels, body(): pl.pallas_call(kernel, name='major_cycle', out_shape=(jax.ShapeDtypeStruc...  74.6 us
    unnamed x3, local copies, waits for them, and re-layouts  4.8 us

profile of v1, /device:TPU:0, one launch (start us, length us, event | category | flops | bytes accessed | tf_op | source)
XLA Modules:
  0.0 80.0 jit_solution(4855887472819112945)
XLA Ops:
  0.6 1.3 %copy.7.lists = s32[8,2]{1,0:T(8,128)} copy(s32[8,2]{0,1:T(2,128)} %param.9) | data formatting | bytes 128 | tf_op args[4]
  2.0 74.6 %major_cycle.1 = (f32[16,2048]{1,0:T(8,128)}, bf16[8,2,128,128]{3,2,1,0:T(8,128)(2,1)}) custom-call(bf16[16,2048]{1,0:T(8,128)(2,1)} %model.1, bf16[8,2,128,128]{3,2,1,0:T(8,128)(2,1)} %observed.1, s32[8]{0:T(128)} %u_off.1, s32[8]{0:T(128)} %v_off.1, s32[8,2]{1,0:T(8,128)} %copy.7.lists), custom_call_target="tpu_custom_call" | custom-call | tf_op jit(solution)/shard_map/major_cycle/pallas_call | solution.py:302
  76.6 1.6 %copy.10 = f32[16,2048]{1,0:T(8,128)} copy(f32[16,2048]{1,0:T(8,128)} %get-tuple-element.4) | data formatting | bytes 262144
  78.2 1.9 %copy.11 = bf16[8,2,128,128]{3,2,1,0:T(8,128)(2,1)} copy(bf16[8,2,128,128]{3,2,1,0:T(8,128)(2,1)} %get-tuple-element.5) | data formatting | bytes 1048576

commit v2 on v1

--- a/solution.py
+++ b/solution.py
@@ -47,9 +47,9 @@
 
 def kernel(
     model, observed, u_off, v_off, lists, dirty, residual,
-    image, uv_out, uv_in, e_c, e_s, g_c, g_s, pv_c, pv_s, pu_c, pu_s, cv, cu, cut,
+    obs_v, image, uv_out, uv_in, e_c, e_s, g_c, g_s, pv_c, pv_s, pu_c, pu_s, cv, cu, cut,
     p_out, p_in, r_out, r_in, total, d_out, d_in,
-    ag_ss, ag_rs, uv_ss, uv_rs, p_ss, p_rs, r_ss, r_rs, d_ss, d_rs,
+    ag_ss, ag_rs, uv_ss, uv_rs, p_ss, p_rs, r_ss, r_rs, d_ss, d_rs, io,
 ):
     f = lax.axis_index("facet")
     j = lax.axis_index("vis")
@@ -60,26 +60,63 @@
     def other_vis(k):
         return {"facet": f, "vis": k}
 
+    def rows(k):
+        return pl.ds(pl.multiple_of(k * ROWS, ROWS), ROWS)
+
+    load_model = pltpu.make_async_copy(model, image.at[rows(j), :], io.at[0])
+    load_observed = pltpu.make_async_copy(observed, obs_v, io.at[1])
+    load_model.start()
+    load_observed.start()
+
+    flip = lax.rem(f, 2) == 1
+    first_at = lax.select(flip, j // 4, lax.rem(j, 4))
+    second_at = lax.select(flip, lax.rem(j, 4), j // 4)
+
+    def place(da, db):
+        a = lax.rem(first_at + da, 4)
+        b = lax.rem(second_at + db, 4)
+        return lax.select(flip, a * 4 + b, b * 4 + a)
+
     barrier = pltpu.get_barrier_semaphore()
-    for d in range(1, NV):
-        pl.semaphore_signal(barrier, inc=1, device_id=other_vis(lax.rem(j + d, NV)), device_id_type=MESH)
+    for d in range(1, 4):
+        pl.semaphore_signal(barrier, inc=1, device_id=other_vis(place(d, 0)), device_id_type=MESH)
+        pl.semaphore_signal(barrier, inc=1, device_id=other_vis(place(0, d)), device_id_type=MESH)
     for d in range(1, NF):
         pl.semaphore_signal(barrier, inc=1, device_id=other_facet(lax.rem(f + d, NF)), device_id_type=MESH)
-    pl.semaphore_wait(barrier, NV - 1 + NF - 1)
+    pl.semaphore_wait(barrier, 6 + NF - 1)
 
     def remote(src, dst, ss, rs, device):
         return pltpu.make_async_remote_copy(
             src_ref=src, dst_ref=dst, send_sem=ss, recv_sem=rs, device_id=device, device_id_type=MESH
         )
 
-    def ag_copy(sender, target):
-        return remote(
-            model, image.at[pl.ds(pl.multiple_of(sender * ROWS, ROWS), ROWS), :],
-            ag_ss.at[target], ag_rs.at[sender], other_vis(target),
-        )
+    def ag_copy(da, ta, tb):
+        owner = place(da, 0)
+        return remote(
+            image.at[rows(owner), :], image.at[rows(owner), :],
+            ag_ss.at[da, ta + tb], ag_rs.at[owner], other_vis(place(ta, tb)),
+        )
+
+    def ag_wait(da, db):
+        owner = place(da, db)
+        remote(
+            image.at[rows(owner), :], image.at[rows(owner), :],
+            ag_ss.at[0, 0], ag_rs.at[owner], other_vis(owner),
+        ).wait_recv()
+
+    def ag_own(d):
+        return remote(
+            image.at[rows(j), :], image.at[rows(j), :], ag_ss.at[0, 3 + d], ag_rs.at[j], other_vis(place(d, 0))
+        )
+
+    load_model.wait()
+    for d in (2, 1, 3):
+        ag_own(d).start()
+    for d in (2, 1, 3):
+        ag_copy(0, 0, d).start()
 
     first, last = [], []
-    hits = [[lists[g, k] for k in range(2)] for g in range(G)]
+    hits = [[lists[k, g] for k in range(2)] for g in range(G)]
     for h in range(NF):
         lo, hi = jnp.int32(0), jnp.int32(0)
         for g in range(G):
@@ -112,11 +149,6 @@
     def _(i):
         uv_copy(f, far_first(i)).start()
 
-    @pl.loop(1, NV)
-    def _(d):
-        ag_copy(j, lax.rem(j + d, NV)).start()
-
-    image[pl.ds(pl.multiple_of(j * ROWS, ROWS), ROWS), :] = model[...]
     uv_in[f] = uv_out[f]
 
     lane = iota((S, LANES), 1)
@@ -133,6 +165,11 @@
         c, s = sincos((sub * (f * STEP + r * LANES + lane)) & (IMG - 1))
         g_c[r] = c
         g_s[r] = s
+
+    for da in (1, 3, 2):
+        ag_wait(da, 0)
+        for d in (2, 1, 3):
+            ag_copy(da, 0, d).start()
 
     @pl.loop(0, NF - 1)
     def _(i):
@@ -155,14 +192,19 @@
 
     @pl.loop(0, 2 * NF)
     def _(n):
+        h = n // 2
+        base = lax.rem(n, 2) * (2 * S)
+        cos_rows = pl.ds(pl.multiple_of(base, S), S)
+        sin_rows = pl.ds(pl.multiple_of(base + S, S), S)
+
         @pl.loop(0, YC)
         def _(r):
             pc = pv_c[n, pl.ds(r, 1), :]
             ps = pv_s[n, pl.ds(r, 1), :]
             ec, es = e_c[r], e_s[r]
             at = pl.ds(pl.multiple_of(r * LANES, LANES), LANES)
-            cv[n, 0:S, at] = (pc * ec - ps * es).astype(BF16)
-            cv[n, S : 2 * S, at] = (ps * ec + pc * es).astype(BF16)
+            cv[h, cos_rows, at] = (pc * ec - ps * es).astype(BF16)
+            cv[h, sin_rows, at] = (ps * ec + pc * es).astype(BF16)
 
         for r in range(XC):
             pc = pu_c[n, r : r + 1, :]
@@ -176,16 +218,16 @@
             cut[n, at, 0:S] = c.T.astype(BF16)
             cut[n, at, S : 2 * S] = s.T.astype(BF16)
 
-    @pl.loop(1, NV)
-    def _(d):
-        k = lax.rem(j + d, NV)
-        ag_copy(k, k).wait_recv()
+    for db in range(1, 4):
+        for da in range(4):
+            ag_wait(da, db)
 
     def predict(h):
+        t = lax.dot_general(cv[h], image[...], NT, preferred_element_type=F32).astype(BF16)
         for s in range(2):
-            n = 2 * h + s
-            t = lax.dot_general(cv[n], image[...], NT, preferred_element_type=F32).astype(BF16)
-            o = lax.dot_general(cu[n], t, NT, preferred_element_type=F32)
+            o = lax.dot_general(
+                cu[2 * h + s], t[2 * S * s : 2 * S * (s + 1)], NT, preferred_element_type=F32
+            )
             yield s, (o[0:S, 0:S] - o[S:, S:]).astype(BF16), (-(o[S:, 0:S] + o[0:S, S:])).astype(BF16)
 
     def p_copy(sender, target):
@@ -211,8 +253,10 @@
     def _(i):
         p_copy(far_first(i), far_first(i)).wait_recv()
 
+    load_observed.wait()
+
     for g in range(G):
-        acc = observed[g].astype(F32)
+        acc = obs_v[g].astype(F32)
         for k in range(2):
             h = hits[g][k]
             slot = jnp.int32(0)
@@ -242,43 +286,53 @@
 
     @pl.loop(0, NF)
     def _(i):
-        h = far_first(NF - 1 - i)
+        h = far_first(lax.select(i < 2, NF - 1 - i, i - 2))
 
         @pl.when(i > 0)
         def _():
             r_copy(h, h).wait_recv()
 
+        z = []
         for s in range(2):
-            n = 2 * h + s
-            re = r_in[n, 0]
-            im = r_in[n, 1]
+            re = r_in[2 * h + s, 0]
+            im = r_in[2 * h + s, 1]
             top = jnp.concatenate([re, -im], axis=1)
             bottom = jnp.concatenate([-im, -re], axis=1)
             both = jnp.concatenate([top, bottom], axis=0)
-            z = lax.dot_general(cut[n], both, NN, preferred_element_type=F32).astype(BF16)
-            total[...] += lax.dot_general(z, cv[n], NN, preferred_element_type=F32)
-
-    def d_copy(sender, target):
-        return remote(d_out.at[target], d_in.at[sender], d_ss.at[target], d_rs.at[sender], other_vis(target))
-
-    @pl.loop(0, NV)
-    def _(k):
-        d_out[k] = total[pl.ds(pl.multiple_of(k * ROWS, ROWS), ROWS), :].astype(BF16)
-
-    @pl.loop(1, NV)
-    def _(d):
-        d_copy(j, lax.rem(j + d, NV)).start()
-
-    acc = total[pl.ds(pl.multiple_of(j * ROWS, ROWS), ROWS), :]
-    dirty[...] = acc
-
-    @pl.loop(1, NV)
-    def _(d):
-        k = lax.rem(j + d, NV)
-        d_copy(k, k).wait_recv()
-        dirty[...] += d_in[k].astype(F32)
-
-    dirty[...] = dirty[...] * F32(1.0 / (S * S))
+            z.append(lax.dot_general(cut[2 * h + s], both, NN, preferred_element_type=F32).astype(BF16))
+        total[...] += lax.dot_general(jnp.concatenate(z, axis=1), cv[h], NN, preferred_element_type=F32)
+
+    def d_copy(da, db):
+        return remote(
+            d_out.at[db, da], d_in.at[4 - db, da], d_ss.at[db, da], d_rs.at[4 - db, da], other_vis(place(0, db))
+        )
+
+    def s_copy(da):
+        return remote(
+            d_out.at[0, da], d_in.at[0, 4 - da], d_ss.at[0, da], d_rs.at[0, 4 - da], other_vis(place(da, 0))
+        )
+
+    for da in (2, 1, 3, 0):
+        for db in (2, 1, 3):
+            d_out[db, da] = total[rows(place(da, db)), :].astype(BF16)
+            d_copy(da, db).start()
+
+    def gathered(da):
+        acc = total[rows(place(da, 0)), :]
+        for db in range(1, 4):
+            d_copy(da, 4 - db).wait_recv()
+            acc = acc + d_in[db, da].astype(F32)
+        return acc
+
+    for da in (2, 1, 3):
+        d_out[0, da] = gathered(da).astype(BF16)
+        s_copy(da).start()
+
+    acc = gathered(0)
+    for da in (2, 1, 3):
+        s_copy(4 - da).wait_recv()
+        acc = acc + d_in[0, da].astype(F32)
+    dirty[...] = acc * F32(1.0 / (S * S))
 
     @pl.loop(0, NF - 1)
     def _(i):
@@ -287,28 +341,27 @@
         p_copy(f, h).wait_send()
         r_copy(f, h).wait_send()
 
-    @pl.loop(1, NV)
-    def _(d):
-        k = lax.rem(j + d, NV)
-        ag_copy(j, k).wait_send()
-        d_copy(j, k).wait_send()
+    for d in range(1, 4):
+        ag_own(d).wait_send()
+        s_copy(d).wait_send()
+        for da in range(4):
+            ag_copy(da, 0, d).wait_send()
+            d_copy(da, d).wait_send()
 
 
 def body(model, observed, u_offsets, v_offsets, facet_lists):
+    hbm = pl.BlockSpec(memory_space=pl.ANY)
     vm = pl.BlockSpec(memory_space=pltpu.VMEM)
     sm = pl.BlockSpec(memory_space=pltpu.SMEM)
     dma = pltpu.SemaphoreType.DMA
-    return tuple(
-        pl.pallas_call(
+    return tuple(pl.pallas_call(
             kernel,
             name="major_cycle",
-            out_shape=(
-                jax.ShapeDtypeStruct((ROWS, FW), F32),
-                jax.ShapeDtypeStruct((G, 2, S, S), BF16),
-            ),
-            in_specs=[vm, vm, sm, sm, sm],
+            out_shape=(pltpu.VMEM((ROWS, FW), F32), pltpu.VMEM((G, 2, S, S), BF16)),
+            in_specs=[hbm, hbm, sm, sm, sm],
             out_specs=(vm, vm),
             scratch_shapes=[
+                pltpu.VMEM((G, 2, S, S), BF16),
                 pltpu.VMEM((FRT, FW), BF16),
                 pltpu.VMEM((NF, 8, LANES), jnp.int32),
                 pltpu.VMEM((NF, 8, LANES), jnp.int32),
@@ -320,7 +373,7 @@
                 pltpu.VMEM((2 * NF, YC, LANES), F32),
                 pltpu.VMEM((2 * NF, 8, LANES), F32),
                 pltpu.VMEM((2 * NF, 8, LANES), F32),
-                pltpu.VMEM((2 * NF, 2 * S, FW), BF16),
+                pltpu.VMEM((NF, 4 * S, FW), BF16),
                 pltpu.VMEM((2 * NF, 2 * S, FRT), BF16),
                 pltpu.VMEM((2 * NF, FRT, 2 * S), BF16),
                 pltpu.VMEM((NF, 2, 2, S, S), BF16),
@@ -328,16 +381,15 @@
                 pltpu.VMEM((2 * NF, 2, S, S), BF16),
                 pltpu.VMEM((2 * NF, 2, S, S), BF16),
                 pltpu.VMEM((FRT, FW), F32),
-                pltpu.VMEM((NV, ROWS, FW), BF16),
-                pltpu.VMEM((NV, ROWS, FW), BF16),
-                dma((NV,)), dma((NV,)), dma((NF,)), dma((NF,)), dma((NF,)), dma((NF,)),
-                dma((NF,)), dma((NF,)), dma((NV,)), dma((NV,)),
+                pltpu.VMEM((4, 4, ROWS, FW), BF16),
+                pltpu.VMEM((4, 4, ROWS, FW), BF16),
+                dma((4, 8)), dma((NV,)), dma((NF,)), dma((NF,)), dma((NF,)), dma((NF,)),
+                dma((NF,)), dma((NF,)), dma((4, 4)), dma((4, 4)), dma((2,)),
             ],
             compiler_params=pltpu.CompilerParams(
                 collective_id=0, has_side_effects=True, vmem_limit_bytes=56 << 20
             ),
-        )(model, observed, u_offsets, v_offsets, facet_lists)
-    )
+        )(model, observed, u_offsets, v_offsets, facet_lists.T))
 
 
 def solution(mesh):

time: 81 us -> 66.5 us (0.82)
  Pallas kernels: 74.6 us -> 63.6 us
  local copies, waits for them, and re-layouts: 4.8 us -> 1.45 us
    pallas_call x1, Pallas kernels: 74.6 us -> 63.6 us  [body(): pl.pallas_call(kernel, name='major_cycle', out_shape=(pltpu.VMEM((ROWS, F...]
    unnamed x3 -> x2, local copies, waits for them, and re-layouts: 4.8 us -> 1.45 us
where the time goes in v2:
time: 66.5 us; the launch traced here: 65.7 us
  Pallas kernels  63.6 us (96%)
  local copies, waits for them, and re-layouts  1.45 us (2%)
    pallas_call x1, Pallas kernels, body(): pl.pallas_call(kernel, name='major_cycle', out_shape=(pltpu.VMEM((ROWS, F...  63.6 us
    unnamed x2, local copies, waits for them, and re-layouts  1.45 us

profile of v2, /device:TPU:0, one launch (start us, length us, event | category | flops | bytes accessed | tf_op | source)
XLA Modules:
  0.0 65.7 jit_solution(2549714637787904861)
XLA Ops:
  0.6 63.6 %major_cycle.1 = (f32[16,2048]{1,0:T(8,128)S(1)}, bf16[8,2,128,128]{3,2,1,0:T(8,128)(2,1)S(1)}) custom-call(bf16[16,2048]{1,0:T(8,128)(2,1)} %model.1, bf16[8,2,128,128]{3,2,1,0:T(8,128)(2,1)} %observed.1, s32[8]{0:T(128)} %u_off.1, s32[8]{0:T(128)} %v_off.1, s32[2,8]{1,0:T(2,128)} %bitcast.1), custom_call_target="tpu_custom_call" | custom-call | tf_op jit(solution)/shard_map/major_cycle/pallas_call | solution.py:357
  64.3 0.7 %copy.9 = f32[16,2048]{1,0:T(8,128)} copy(f32[16,2048]{1,0:T(8,128)S(1)} %get-tuple-element.2) | data formatting | bytes 262144
  64.9 0.8 %copy.10 = bf16[8,2,128,128]{3,2,1,0:T(8,128)(2,1)} copy(bf16[8,2,128,128]{3,2,1,0:T(8,128)(2,1)S(1)} %get-tuple-element.3) | data formatting | bytes 1048576

commit v3 on v2

v3 whole, which is shorter than its diff:
```python
import math

import jax
import jax.numpy as jnp
from jax import lax
from jax.experimental import pallas as pl
from jax.experimental.pallas import tpu as pltpu
from jax.sharding import PartitionSpec as P

IMG = 32768
LANES = 128
NF = 8
NV = 16
S = 128
FW = 2048
FRT = 256
ROWS = 16
G = 8
YC = FW // LANES
XC = FRT // LANES
STEP = IMG // NF
MESH = pl.DeviceIdType.MESH
F32 = jnp.float32
BF16 = jnp.bfloat16
NT = (((1,), (1,)), ((), ()))
NN = (((1,), (0,)), ((), ()))


def sincos(index):
    quarter = (index + IMG // 8) >> 13
    rest = index - (quarter << 13)
    angle = rest.astype(F32) * F32(2.0 * math.pi / IMG)
    t = angle * angle
    sn = angle * (1.0 + t * (-1.0 / 6 + t * (1.0 / 120 + t * (-1.0 / 5040 + t * (1.0 / 362880)))))
    cs = 1.0 + t * (-0.5 + t * (1.0 / 24 + t * (-1.0 / 720 + t * (1.0 / 40320))))
    odd = (quarter & 1) == 1
    c = jnp.where(odd, sn, cs)
    s = jnp.where(odd, cs, sn)
    c = jnp.where(((quarter + 1) & 2) != 0, -c, c)
    s = jnp.where((quarter & 2) != 0, -s, s)
    return c, s


def iota(shape, axis):
    return lax.broadcasted_iota(jnp.int32, shape, axis)


def kernel(
    model, observed, u_hbm, v_hbm, lists_hbm, dirty, residual,
    u_off, v_off, lists, obs_v, image, uv_out, uv_in, e_c, e_s, g_c, g_s, pv_c, pv_s, pu_c, pu_s, cv, cu, cut,
    p_out, p_in, r_out, r_in, total, d_out, d_in,
    ag_ss, ag_rs, uv_ss, uv_rs, p_ss, p_rs, r_ss, r_rs, d_ss, d_rs, hop_ss, hop_rs, up_ss, up_rs, io,
):
    f = lax.axis_index("facet")
    j = lax.axis_index("vis")
    z = f // 2
    c = lax.rem(f, 2)
    far = lax.rem(f + NF // 2, NF)

    def rows(k, which=0):
        return pl.ds(pl.multiple_of(which * FRT + k * ROWS, ROWS), ROWS)

    def remote(src, dst, ss, rs, device):
        return pltpu.make_async_remote_copy(
            src_ref=src, dst_ref=dst, send_sem=ss, recv_sem=rs, device_id=device, device_id_type=MESH
        )

    def other_facet(h):
        return {"facet": h, "vis": j}

    def other_vis(k):
        return {"facet": f, "vis": k}

    def along(q, last_dz):
        return jnp.where(q == 0, 1, jnp.where(q == 1, 3, jnp.where(q == 2, 0, last_dz)))

    def facet_of(p):
        return lax.rem(z + along(p // 2, 2), 4) * 2 + lax.rem(c + lax.rem(p, 2), 2)

    def home_of(p):
        return lax.rem(z + along(p // 2, 0), 4) * 2 + lax.rem(c + lax.rem(p, 2), 2)

    def back(p):
        return jnp.where(p < 2, p + 2, jnp.where(p < 4, p - 2, p))

    def z_first(i):
        return jnp.where(i < 4, 2 * lax.rem(i, 2) + i // 2, i + 1 - 2 * lax.rem(i, 2))

    def two_first(i):
        return jnp.where(i == 0, 2, jnp.where(i == 1, 1, jnp.where(i == 2, 3, 0)))

    load_model = pltpu.make_async_copy(model, image.at[rows(j), :], io.at[0])
    load_observed = pltpu.make_async_copy(observed, obs_v, io.at[1])
    load_small = [
        pltpu.make_async_copy(src, dst, io.at[2 + i])
        for i, (src, dst) in enumerate(((u_hbm, u_off), (v_hbm, v_off), (lists_hbm, lists)))
    ]
    load_model.start()
    for load in load_small:
        load.start()
    load_observed.start()

    flip = c == 1
    first_at = lax.select(flip, j // 4, lax.rem(j, 4))
    second_at = lax.select(flip, lax.rem(j, 4), j // 4)

    def place(da, db):
        a = lax.rem(first_at + da, 4)
        b = lax.rem(second_at + db, 4)
        return lax.select(flip, a * 4 + b, b * 4 + a)

    barrier = pltpu.get_barrier_semaphore()
    for d in range(1, 4):
        pl.semaphore_signal(barrier, inc=1, device_id=other_vis(place(d, 0)), device_id_type=MESH)
        pl.semaphore_signal(barrier, inc=1, device_id=other_vis(place(0, d)), device_id_type=MESH)
    for p in (0, 1, 2, 3, 5):
        pl.semaphore_signal(barrier, inc=1, device_id=other_facet(home_of(p)), device_id_type=MESH)
    pl.semaphore_signal(barrier, inc=1, device_id=other_facet(far), device_id_type=MESH)
    pl.semaphore_wait(barrier, 12)

    def ag_copy(w, da, ta, tb):
        block = image.at[rows(place(da, 0), w), :]
        return remote(
            block, block, ag_ss.at[w, da, ta + 4 * tb], ag_rs.at[w, da, 0 if tb == 0 else 4 - tb]
            if ta == 0 else ag_rs.at[w, 4 - ta, 0], other_vis(place(ta, tb)),
        )

    def ag_wait(w, da, db):
        block = image.at[rows(place(da, db), w), :]
        remote(block, block, ag_ss.at[w, 0, 0], ag_rs.at[w, da, db], other_vis(place(1, 0))).wait_recv()

    def ag_second(w, da):
        for d in (2, 1, 3):
            ag_copy(w, da, 0, d).start()

    def ag_rest(w):
        for db in range(1, 4):
            for da in range(4):
                ag_wait(w, da, db)

    def model_hop(da):
        at = place(da, 0)
        return remote(
            image.at[rows(at), :], image.at[rows(at, 1), :], hop_ss.at[da], hop_rs.at[da], other_facet(far)
        )

    load_model.wait()
    for d in (2, 1, 3):
        ag_copy(0, 0, d, 0).start()
    ag_second(0, 0)
    model_hop(0).start()

    for load in load_small:
        load.wait()

    def listed(h):
        lo, hi = jnp.int32(0), jnp.int32(0)
        for g in range(G):
            hi = jnp.where((lists[0, g] == h) | (lists[1, g] == h), g, hi)
        for g in reversed(range(G)):
            lo = jnp.where((lists[0, g] == h) | (lists[1, g] == h), g, lo)
        return lo, hi

    row = iota((8, LANES), 0)

    @pl.loop(0, 6)
    def _(p):
        tile = jnp.zeros((8, LANES), jnp.int32)
        for half in range(2):
            lo, hi = listed(facet_of(jnp.minimum(p + 2 * half, NF - 1)))
            for at, value in enumerate((u_off[lo], u_off[hi], v_off[lo], v_off[hi])):
                tile = jnp.where(row == 4 * half + at, value, tile)
        uv_out[p] = tile

    def uv_copy(p):
        return remote(uv_out.at[p], uv_in.at[back(p)], uv_ss.at[p], uv_rs.at[back(p)], other_facet(home_of(p)))

    for p in (0, 1, 2, 3, 5):
        uv_copy(p).start()
    uv_in[4] = uv_out[4]

    lane = iota((S, LANES), 1)
    sub = iota((S, LANES), 0)

    @pl.loop(0, XC)
    def _(r):
        for w, facet in enumerate((f, far)):
            co, si = sincos((sub * (facet * STEP + r * LANES + lane)) & (IMG - 1))
            g_c[w, r] = co
            g_s[w, r] = si

    @pl.loop(0, YC)
    def _(r):
        co, si = sincos((sub * (r * LANES + lane)) & (IMG - 1))
        e_c[r] = co
        e_s[r] = si

    for da in (1, 3, 2):
        ag_wait(0, da, 0)
        ag_second(0, da)
        model_hop(da).start()

    for p in (0, 1, 2, 3, 5):
        uv_copy(back(p)).wait_recv()

    y_of = iota((YC, LANES), 0) * LANES + iota((YC, LANES), 1)
    x_of = iota((8, LANES), 0) * LANES + iota((8, LANES), 1)

    @pl.loop(0, 2 * NF)
    def _(n):
        p = n // 2
        w = p // 6
        at = 4 * w + lax.rem(n, 2)
        u = uv_in[p - 2 * w, pl.ds(at, 1), :]
        v = uv_in[p - 2 * w, pl.ds(at + 2, 1), :]
        co, si = sincos((v * y_of) & (IMG - 1))
        pv_c[n] = co
        pv_s[n] = si
        co, si = sincos((u * (x_of + jnp.where(w == 1, far, f) * STEP)) & (IMG - 1))
        pu_c[n] = co
        pu_s[n] = si

    @pl.loop(0, 2 * NF)
    def _(n):
        p = n // 2
        w = p // 6
        base = lax.rem(n, 2) * (2 * S)
        cos_rows = pl.ds(pl.multiple_of(base, S), S)
        sin_rows = pl.ds(pl.multiple_of(base + S, S), S)

        @pl.loop(0, YC)
        def _(r):
            pc = pv_c[n, pl.ds(r, 1), :]
            ps = pv_s[n, pl.ds(r, 1), :]
            ec, es = e_c[r], e_s[r]
            at = pl.ds(pl.multiple_of(r * LANES, LANES), LANES)
            cv[p, cos_rows, at] = (pc * ec - ps * es).astype(BF16)
            cv[p, sin_rows, at] = (ps * ec + pc * es).astype(BF16)

        @pl.loop(0, XC)
        def _(r):
            pc = pu_c[n, pl.ds(r, 1), :]
            ps = pu_s[n, pl.ds(r, 1), :]
            ec, es = g_c[w, r], g_s[w, r]
            at = pl.ds(pl.multiple_of(r * LANES, LANES), LANES)
            co = pc * ec - ps * es
            si = ps * ec + pc * es
            cu[n, 0:S, at] = co.astype(BF16)
            cu[n, S : 2 * S, at] = si.astype(BF16)
            cut[n, at, 0:S] = co.T.astype(BF16)
            cut[n, at, S : 2 * S] = si.T.astype(BF16)

    total[...] = jnp.zeros_like(total)
    ag_rest(0)

    def p_copy(p, s):
        return remote(
            p_out.at[2 * p + s], p_in.at[2 * back(p) + s],
            p_ss.at[2 * p + s], p_rs.at[2 * back(p) + s], other_facet(home_of(p)),
        )

    @pl.loop(0, NF)
    def _(i):
        p = z_first(i)

        @pl.when(i == 1)
        def _():
            for da in (0, 1, 3, 2):
                model_hop(da).wait_recv()
                ag_second(1, da)

        @pl.when(i == 6)
        def _():
            ag_rest(1)

        window = pl.ds(pl.multiple_of(p // 6 * FRT, FRT), FRT)
        t = lax.dot_general(cv[p], image[window, :], NT, preferred_element_type=F32).astype(BF16)
        for s in range(2):
            o = lax.dot_general(
                cu[2 * p + s], t[2 * S * s : 2 * S * (s + 1)], NT, preferred_element_type=F32
            )
            p_out[2 * p + s, 0] = (o[0:S, 0:S] - o[S:, S:]).astype(BF16)
            p_out[2 * p + s, 1] = (-(o[S:, 0:S] + o[0:S, S:])).astype(BF16)

            @pl.when((i != 5) & (i != 7))
            def _():
                p_copy(p, s).start()

    for n in (8, 9, 12, 13):
        p_in[n] = p_out[n]

    load_observed.wait()
    for p in (0, 1, 2, 3, 5, 7):
        for s in range(2):
            p_copy(back(p), s).wait_recv()

    @pl.loop(0, G)
    def _(g):
        acc = obs_v[g].astype(F32)
        for k in range(2):
            h = lists[k, g]
            slot = jnp.int32(0)
            for e in range(G):
                slot = jnp.where((e < g) & ((lists[0, e] == h) | (lists[1, e] == h)), 1, slot)
            dz = (h // 2 - z) & 3
            q = jnp.where(dz == 0, 2, jnp.where(dz == 1, 0, jnp.where(dz == 2, 3, 1)))
            acc = acc - p_in[4 * q + 2 * ((h - c) & 1) + slot].astype(F32)
        residual[g] = acc.astype(BF16)

    def r_copy(p):
        return remote(
            r_out.at[pl.ds(2 * p, 2)], r_in.at[pl.ds(2 * back(p), 2)],
            r_ss.at[p], r_rs.at[back(p)], other_facet(home_of(p)),
        )

    @pl.loop(0, NF)
    def _(i):
        p = z_first(i)
        lo, hi = listed(facet_of(p))
        r_out[2 * p] = residual[lo]
        r_out[2 * p + 1] = residual[hi]

        @pl.when((i < 2) | (i == 4) | (i == 6))
        def _():
            r_copy(p).start()

    for n in (8, 9, 12, 13):
        r_in[n] = r_out[n]

    def d_copy(w, da, db):
        return remote(
            d_out.at[w, db, da], d_in.at[w, 4 - db, da], d_ss.at[w, db, da], d_rs.at[w, 4 - db, da],
            other_vis(place(0, db)),
        )

    def s_copy(da):
        return remote(
            d_out.at[0, 0, da], d_in.at[0, 0, 4 - da], d_ss.at[0, 0, da], d_rs.at[0, 0, 4 - da],
            other_vis(place(da, 0)),
        )

    def image_hop(da):
        return remote(d_out.at[1, 0, da], d_in.at[1, 0, da], up_ss.at[da], up_rs.at[da], other_facet(far))

    def spread(w):
        @pl.loop(0, 12)
        def _(i):
            da = two_first(i // 3)
            db = two_first(lax.rem(i, 3))
            d_out[w, db, da] = total[w, rows(place(da, db)), :].astype(BF16)
            d_copy(w, da, db).start()

    def gathered(w, da):
        acc = total[w, rows(place(da, 0)), :]
        for db in range(1, 4):
            d_copy(w, da, 4 - db).wait_recv()
            acc = acc + d_in[w, db, da].astype(F32)
        return acc

    def both_chips(da):
        acc = gathered(0, da)
        image_hop(da).wait_recv()
        return acc + d_in[1, 0, da].astype(F32)

    @pl.loop(0, NF)
    def _(i):
        p = jnp.where(i < 2, i + 6, jnp.where(i < 4, i + 2, z_first(i - 4)))
        w = jnp.where(i < 2, 1, 0)

        @pl.when(i == 1)
        def _():
            for unit in (1, 3):
                r_copy(unit).start()

        @pl.when(i == 2)
        def _():
            spread(1)

        @pl.when((i != 0) & (i != 2))
        def _():
            r_copy(back(p)).wait_recv()

        zs = []
        for s in range(2):
            re = r_in[2 * p + s, 0]
            im = r_in[2 * p + s, 1]
            top = jnp.concatenate([re, -im], axis=1)
            bottom = jnp.concatenate([-im, -re], axis=1)
            both = jnp.concatenate([top, bottom], axis=0)
            zs.append(lax.dot_general(cut[2 * p + s], both, NN, preferred_element_type=F32).astype(BF16))
        total[w] += lax.dot_general(jnp.concatenate(zs, axis=1), cv[p], NN, preferred_element_type=F32)

    spread(0)

    @pl.loop(0, 4)
    def _(i):
        da = two_first(i)
        d_out[1, 0, da] = gathered(1, da).astype(BF16)
        image_hop(da).start()

    @pl.loop(0, 3)
    def _(i):
        da = two_first(i)
        d_out[0, 0, da] = both_chips(da).astype(BF16)
        s_copy(da).start()

    acc = both_chips(0)
    for da in (2, 1, 3):
        s_copy(4 - da).wait_recv()
        acc = acc + d_in[0, 0, da].astype(F32)
    dirty[...] = acc * F32(1.0 / (S * S))

    for p in (0, 1, 2, 3, 5):
        uv_copy(p).wait_send()
    for p in (0, 1, 2, 3, 5, 7):
        r_copy(p).wait_send()
        for s in range(2):
            p_copy(p, s).wait_send()
    for da in range(4):
        model_hop(da).wait_send()
        image_hop(da).wait_send()
        for d in range(1, 4):
            for w in range(2):
                ag_copy(w, da, 0, d).wait_send()
                d_copy(w, da, d).wait_send()
    for d in range(1, 4):
        ag_copy(0, 0, d, 0).wait_send()
        s_copy(d).wait_send()


def body(model, observed, u_offsets, v_offsets, facet_lists):
    hbm = pl.BlockSpec(memory_space=pl.ANY)
    vm = pl.BlockSpec(memory_space=pltpu.VMEM)
    dma = pltpu.SemaphoreType.DMA
    return tuple(pl.pallas_call(
            kernel,
            name="major_cycle",
            out_shape=(pltpu.VMEM((ROWS, FW), F32), pltpu.VMEM((G, 2, S, S), BF16)),
            in_specs=[hbm] * 5,
            out_specs=(vm, vm),
            scratch_shapes=[
                pltpu.SMEM((G,), jnp.int32),
                pltpu.SMEM((G,), jnp.int32),
                pltpu.SMEM((2, G), jnp.int32),
                pltpu.VMEM((G, 2, S, S), BF16),
                pltpu.VMEM((2 * FRT, FW), BF16),
                pltpu.VMEM((6, 8, LANES), jnp.int32),
                pltpu.VMEM((6, 8, LANES), jnp.int32),
                pltpu.VMEM((YC, S, LANES), F32),
                pltpu.VMEM((YC, S, LANES), F32),
                pltpu.VMEM((2, XC, S, LANES), F32),
                pltpu.VMEM((2, XC, S, LANES), F32),
                pltpu.VMEM((2 * NF, YC, LANES), F32),
                pltpu.VMEM((2 * NF, YC, LANES), F32),
                pltpu.VMEM((2 * NF, 8, LANES), F32),
                pltpu.VMEM((2 * NF, 8, LANES), F32),
                pltpu.VMEM((NF, 4 * S, FW), BF16),
                pltpu.VMEM((2 * NF, 2 * S, FRT), BF16),
                pltpu.VMEM((2 * NF, FRT, 2 * S), BF16),
                pltpu.VMEM((2 * NF, 2, S, S), BF16),
                pltpu.VMEM((2 * NF, 2, S, S), BF16),
                pltpu.VMEM((2 * NF, 2, S, S), BF16),
                pltpu.VMEM((2 * NF, 2, S, S), BF16),
                pltpu.VMEM((2, FRT, FW), F32),
                pltpu.VMEM((2, 4, 4, ROWS, FW), BF16),
                pltpu.VMEM((2, 4, 4, ROWS, FW), BF16),
                dma((2, 4, 16)), dma((2, 4, 4)), dma((6,)), dma((6,)), dma((2 * NF,)), dma((2 * NF,)),
                dma((NF,)), dma((NF,)), dma((2, 4, 4)), dma((2, 4, 4)),
                dma((4,)), dma((4,)), dma((4,)), dma((4,)), dma((5,)),
            ],
            compiler_params=pltpu.CompilerParams(
                collective_id=0, has_side_effects=True, vmem_limit_bytes=56 << 20
            ),
        )(model, observed, u_offsets, v_offsets, facet_lists.T))


def solution(mesh):
    in_specs = (
        P(("facet", "vis"), None),
        P(("facet", "vis"), None, None, None),
        P(("facet", "vis")),
        P(("facet", "vis")),
        P(("facet", "vis"), None),
    )
    out_specs = (P(("facet", "vis"), None), P(("facet", "vis"), None, None, None))
    return jax.shard_map(body, mesh=mesh, in_specs=in_specs, out_specs=out_specs, check_vma=False)
```

time: 66.5 us -> 61.7 us (0.928)
  Pallas kernels: 63.6 us -> 59.2 us
    pallas_call x1, Pallas kernels: 63.6 us -> 59.2 us  [body(): pl.pallas_call(kernel, name='major_cycle', out_shape=(pltpu.VMEM((ROWS, F...]
where the time goes in v3:
time: 61.7 us; the launch traced here: 61.3 us
  Pallas kernels  59.2 us (96%)
  local copies, waits for them, and re-layouts  1.45 us (2%)
  between operations  0.64 us (1%)
    pallas_call x1, Pallas kernels, body(): pl.pallas_call(kernel, name='major_cycle', out_shape=(pltpu.VMEM((ROWS, F...  59.2 us
    unnamed x2, local copies, waits for them, and re-layouts  1.45 us

profile of v3, /device:TPU:0, one launch (start us, length us, event | category | flops | bytes accessed | tf_op | source)
XLA Modules:
  0.0 61.3 jit_solution(8622315542149689352)
XLA Ops:
  0.6 59.2 %major_cycle.1 = (f32[16,2048]{1,0:T(8,128)S(1)}, bf16[8,2,128,128]{3,2,1,0:T(8,128)(2,1)S(1)}) custom-call(bf16[16,2048]{1,0:T(8,128)(2,1)} %model.1, bf16[8,2,128,128]{3,2,1,0:T(8,128)(2,1)} %observed.1, s32[8]{0:T(128)} %u_hbm.1, s32[8]{0:T(128)} %v_hbm.1, s32[2,8]{1,0:T(2,128)} %bitcast.1), custom_call_target="tpu_custom_call" | custom-call | tf_op jit(solution)/shard_map/major_cycle/pallas_call | solution.py:435
  59.8 0.7 %copy.9 = f32[16,2048]{1,0:T(8,128)} copy(f32[16,2048]{1,0:T(8,128)S(1)} %get-tuple-element.2) | data formatting | bytes 262144
  60.5 0.8 %copy.10 = bf16[8,2,128,128]{3,2,1,0:T(8,128)(2,1)} copy(bf16[8,2,128,128]{3,2,1,0:T(8,128)(2,1)S(1)} %get-tuple-element.3) | data formatting | bytes 1048576

commit v4 on v3

--- a/solution.py
+++ b/solution.py
@@ -220,71 +220,83 @@
         pu_c[n] = co
         pu_s[n] = si
 
+    total[...] = jnp.zeros_like(total)
+
+    def p_copy(p, s):
+        return remote(
+            p_out.at[2 * p + s], p_in.at[2 * back(p) + s],
+            p_ss.at[2 * p + s], p_rs.at[2 * back(p) + s], other_facet(home_of(p)),
+        )
+
+    @pl.loop(0, 2)
+    def _(half):
+        @pl.loop(NF * half, NF * half + NF)
+        def _(n):
+            p = n // 2
+            w = p // 6
+            base = lax.rem(n, 2) * (2 * S)
+            cos_rows = pl.ds(pl.multiple_of(base, S), S)
+            sin_rows = pl.ds(pl.multiple_of(base + S, S), S)
+
+            @pl.loop(0, YC, step=16)
+            def _(r0):
+                for k in range(16):
+                    r = r0 + k
+                    pc = pv_c[n, pl.ds(r, 1), :]
+                    ps = pv_s[n, pl.ds(r, 1), :]
+                    ec, es = e_c[r], e_s[r]
+                    at = pl.ds(pl.multiple_of(r * LANES, LANES), LANES)
+                    cv[p, cos_rows, at] = (pc * ec - ps * es).astype(BF16)
+                    cv[p, sin_rows, at] = (ps * ec + pc * es).astype(BF16)
+
+            @pl.loop(0, XC)
+            def _(r):
+                pc = pu_c[n, pl.ds(r, 1), :]
+                ps = pu_s[n, pl.ds(r, 1), :]
+                ec, es = g_c[w, r], g_s[w, r]
+                at = pl.ds(pl.multiple_of(r * LANES, LANES), LANES)
+                co = pc * ec - ps * es
+                si = ps * ec + pc * es
+                cu[n, 0:S, at] = co.astype(BF16)
+                cu[n, S : 2 * S, at] = si.astype(BF16)
+
+        @pl.when(half == 0)
+        def _():
+            ag_rest(0)
+
+        @pl.loop(4 * half, 4 * half + 4)
+        def _(i):
+            p = z_first(i)
+
+            @pl.when(i == 1)
+            def _():
+                for da in (0, 1, 3, 2):
+                    model_hop(da).wait_recv()
+                    ag_second(1, da)
+
+            @pl.when(i == 6)
+            def _():
+                ag_rest(1)
+
+            window = pl.ds(pl.multiple_of(p // 6 * FRT, FRT), FRT)
+            t = lax.dot_general(cv[p], image[window, :], NT, preferred_element_type=F32).astype(BF16)
+            for s in range(2):
+                o = lax.dot_general(
+                    cu[2 * p + s], t[2 * S * s : 2 * S * (s + 1)], NT, preferred_element_type=F32
+                )
+                p_out[2 * p + s, 0] = (o[0:S, 0:S] - o[S:, S:]).astype(BF16)
+                p_out[2 * p + s, 1] = (-(o[S:, 0:S] + o[0:S, S:])).astype(BF16)
+
+                @pl.when((i != 5) & (i != 7))
+                def _():
+                    p_copy(p, s).start()
+
     @pl.loop(0, 2 * NF)
     def _(n):
-        p = n // 2
-        w = p // 6
-        base = lax.rem(n, 2) * (2 * S)
-        cos_rows = pl.ds(pl.multiple_of(base, S), S)
-        sin_rows = pl.ds(pl.multiple_of(base + S, S), S)
-
-        @pl.loop(0, YC)
-        def _(r):
-            pc = pv_c[n, pl.ds(r, 1), :]
-            ps = pv_s[n, pl.ds(r, 1), :]
-            ec, es = e_c[r], e_s[r]
-            at = pl.ds(pl.multiple_of(r * LANES, LANES), LANES)
-            cv[p, cos_rows, at] = (pc * ec - ps * es).astype(BF16)
-            cv[p, sin_rows, at] = (ps * ec + pc * es).astype(BF16)
-
-        @pl.loop(0, XC)
-        def _(r):
-            pc = pu_c[n, pl.ds(r, 1), :]
-            ps = pu_s[n, pl.ds(r, 1), :]
-            ec, es = g_c[w, r], g_s[w, r]
-            at = pl.ds(pl.multiple_of(r * LANES, LANES), LANES)
-            co = pc * ec - ps * es
-            si = ps * ec + pc * es
-            cu[n, 0:S, at] = co.astype(BF16)
-            cu[n, S : 2 * S, at] = si.astype(BF16)
-            cut[n, at, 0:S] = co.T.astype(BF16)
-            cut[n, at, S : 2 * S] = si.T.astype(BF16)
-
-    total[...] = jnp.zeros_like(total)
-    ag_rest(0)
-
-    def p_copy(p, s):
-        return remote(
-            p_out.at[2 * p + s], p_in.at[2 * back(p) + s],
-            p_ss.at[2 * p + s], p_rs.at[2 * back(p) + s], other_facet(home_of(p)),
-        )
-
-    @pl.loop(0, NF)
-    def _(i):
-        p = z_first(i)
-
-        @pl.when(i == 1)
-        def _():
-            for da in (0, 1, 3, 2):
-                model_hop(da).wait_recv()
-                ag_second(1, da)
-
-        @pl.when(i == 6)
-        def _():
-            ag_rest(1)
-
-        window = pl.ds(pl.multiple_of(p // 6 * FRT, FRT), FRT)
-        t = lax.dot_general(cv[p], image[window, :], NT, preferred_element_type=F32).astype(BF16)
-        for s in range(2):
-            o = lax.dot_general(
-                cu[2 * p + s], t[2 * S * s : 2 * S * (s + 1)], NT, preferred_element_type=F32
-            )
-            p_out[2 * p + s, 0] = (o[0:S, 0:S] - o[S:, S:]).astype(BF16)
-            p_out[2 * p + s, 1] = (-(o[S:, 0:S] + o[0:S, S:])).astype(BF16)
-
-            @pl.when((i != 5) & (i != 7))
-            def _():
-                p_copy(p, s).start()
+        for r in range(XC):
+            at = slice(r * LANES, (r + 1) * LANES)
+            for k in range(2):
+                cut[n, at, k * S : (k + 1) * S] = cu[n, k * S : (k + 1) * S, at].T
 
     for n in (8, 9, 12, 13):
         p_in[n] = p_out[n]

time: 61.7 us -> 58 us (0.940)
  Pallas kernels: 59.2 us -> 55.8 us
    pallas_call x1, Pallas kernels: 59.2 us -> 55.8 us  [body(): pl.pallas_call(kernel, name='major_cycle', out_shape=(pltpu.VMEM((ROWS, F...]
where the time goes in v4:
time: 58 us; the launch traced here: 57.9 us
  Pallas kernels  55.8 us (96%)
  local copies, waits for them, and re-layouts  1.45 us (2%)
  between operations  0.64 us (1%)
    pallas_call x1, Pallas kernels, body(): pl.pallas_call(kernel, name='major_cycle', out_shape=(pltpu.VMEM((ROWS, F...  55.8 us
    unnamed x2, local copies, waits for them, and re-layouts  1.45 us

profile of v4, /device:TPU:0, one launch (start us, length us, event | category | flops | bytes accessed | tf_op | source)
XLA Modules:
  0.0 57.9 jit_solution(7518584292543965198)
XLA Ops:
  0.6 55.8 %major_cycle.1 = (f32[16,2048]{1,0:T(8,128)S(1)}, bf16[8,2,128,128]{3,2,1,0:T(8,128)(2,1)S(1)}) custom-call(bf16[16,2048]{1,0:T(8,128)(2,1)} %model.1, bf16[8,2,128,128]{3,2,1,0:T(8,128)(2,1)} %observed.1, s32[8]{0:T(128)} %u_hbm.1, s32[8]{0:T(128)} %v_hbm.1, s32[2,8]{1,0:T(2,128)} %bitcast.1), custom_call_target="tpu_custom_call" | custom-call | tf_op jit(solution)/shard_map/major_cycle/pallas_call | solution.py:447
  56.5 0.7 %copy.9 = f32[16,2048]{1,0:T(8,128)} copy(f32[16,2048]{1,0:T(8,128)S(1)} %get-tuple-element.2) | data formatting | bytes 262144
  57.1 0.8 %copy.10 = bf16[8,2,128,128]{3,2,1,0:T(8,128)(2,1)} copy(bf16[8,2,128,128]{3,2,1,0:T(8,128)(2,1)S(1)} %get-tuple-element.3) | data formatting | bytes 1048576

commit v5 on v3

--- a/solution.py
+++ b/solution.py
@@ -47,7 +47,7 @@
 
 def kernel(
     model, observed, u_hbm, v_hbm, lists_hbm, dirty, residual,
-    u_off, v_off, lists, obs_v, image, uv_out, uv_in, e_c, e_s, g_c, g_s, pv_c, pv_s, pu_c, pu_s, cv, cu, cut,
+    u_off, v_off, lists, obs_v, image, uv_out, uv_in, e_c, e_s, g_c, g_s, pv_c, pv_s, pu_c, pu_s, cv_a, cv_b, cu_a, cu_b, cut,
     p_out, p_in, r_out, r_in, total, d_out, d_in,
     ag_ss, ag_rs, uv_ss, uv_rs, p_ss, p_rs, r_ss, r_rs, d_ss, d_rs, hop_ss, hop_rs, up_ss, up_rs, io,
 ):
@@ -220,38 +220,7 @@
         pu_c[n] = co
         pu_s[n] = si
 
-    @pl.loop(0, 2 * NF)
-    def _(n):
-        p = n // 2
-        w = p // 6
-        base = lax.rem(n, 2) * (2 * S)
-        cos_rows = pl.ds(pl.multiple_of(base, S), S)
-        sin_rows = pl.ds(pl.multiple_of(base + S, S), S)
-
-        @pl.loop(0, YC)
-        def _(r):
-            pc = pv_c[n, pl.ds(r, 1), :]
-            ps = pv_s[n, pl.ds(r, 1), :]
-            ec, es = e_c[r], e_s[r]
-            at = pl.ds(pl.multiple_of(r * LANES, LANES), LANES)
-            cv[p, cos_rows, at] = (pc * ec - ps * es).astype(BF16)
-            cv[p, sin_rows, at] = (ps * ec + pc * es).astype(BF16)
-
-        @pl.loop(0, XC)
-        def _(r):
-            pc = pu_c[n, pl.ds(r, 1), :]
-            ps = pu_s[n, pl.ds(r, 1), :]
-            ec, es = g_c[w, r], g_s[w, r]
-            at = pl.ds(pl.multiple_of(r * LANES, LANES), LANES)
-            co = pc * ec - ps * es
-            si = ps * ec + pc * es
-            cu[n, 0:S, at] = co.astype(BF16)
-            cu[n, S : 2 * S, at] = si.astype(BF16)
-            cut[n, at, 0:S] = co.T.astype(BF16)
-            cut[n, at, S : 2 * S] = si.T.astype(BF16)
-
     total[...] = jnp.zeros_like(total)
-    ag_rest(0)
 
     def p_copy(p, s):
         return remote(
@@ -259,7 +228,47 @@
             p_ss.at[2 * p + s], p_rs.at[2 * back(p) + s], other_facet(home_of(p)),
         )
 
-    @pl.loop(0, NF)
+    def tables(p, s, cv, cu, k):
+        n = 2 * p + s
+        w = p // 6
+        base = 2 * S * s
+        for r in range(YC):
+            pc = pv_c[n, r : r + 1, :]
+            ps = pv_s[n, r : r + 1, :]
+            ec, es = e_c[r], e_s[r]
+            at = slice(r * LANES, (r + 1) * LANES)
+            cv[k, base : base + S, at] = (pc * ec - ps * es).astype(BF16)
+            cv[k, base + S : base + 2 * S, at] = (ps * ec + pc * es).astype(BF16)
+        for r in range(XC):
+            pc = pu_c[n, r : r + 1, :]
+            ps = pu_s[n, r : r + 1, :]
+            ec, es = g_c[w, r], g_s[w, r]
+            at = slice(r * LANES, (r + 1) * LANES)
+            cu[2 * k + s, 0:S, at] = (pc * ec - ps * es).astype(BF16)
+            cu[2 * k + s, S : 2 * S, at] = (ps * ec + pc * es).astype(BF16)
+
+    def predict(p, window, cv, cu, k):
+        t = lax.dot_general(cv[k], image[window, :], NT, preferred_element_type=F32).astype(BF16)
+        for s in range(2):
+            o = lax.dot_general(
+                cu[2 * k + s], t[2 * S * s : 2 * S * (s + 1)], NT, preferred_element_type=F32
+            )
+            p_out[2 * p + s, 0] = (o[0:S, 0:S] - o[S:, S:]).astype(BF16)
+            p_out[2 * p + s, 1] = (-(o[S:, 0:S] + o[0:S, S:])).astype(BF16)
+
+    @pl.loop(0, 4)
+    def _(p):
+        for s in range(2):
+            tables(p, s, cv_a, cu_a, p)
+
+    @pl.loop(0, 4)
+    def _(p):
+        for s in range(2):
+            tables(p + 4, s, cv_b, cu_b, p)
+
+    ag_rest(0)
+
+    @pl.loop(0, 4)
     def _(i):
         p = z_first(i)
 
@@ -269,22 +278,33 @@
                 model_hop(da).wait_recv()
                 ag_second(1, da)
 
+        predict(p, slice(0, FRT), cv_a, cu_a, p)
+        for s in range(2):
+            p_copy(p, s).start()
+
+    @pl.loop(4, NF)
+    def _(i):
+        p = z_first(i)
+
         @pl.when(i == 6)
         def _():
             ag_rest(1)
 
-        window = pl.ds(pl.multiple_of(p // 6 * FRT, FRT), FRT)
-        t = lax.dot_general(cv[p], image[window, :], NT, preferred_element_type=F32).astype(BF16)
-        for s in range(2):
-            o = lax.dot_general(
-                cu[2 * p + s], t[2 * S * s : 2 * S * (s + 1)], NT, preferred_element_type=F32
-            )
-            p_out[2 * p + s, 0] = (o[0:S, 0:S] - o[S:, S:]).astype(BF16)
-            p_out[2 * p + s, 1] = (-(o[S:, 0:S] + o[0:S, S:])).astype(BF16)
-
-            @pl.when((i != 5) & (i != 7))
-            def _():
+        predict(p, pl.ds(pl.multiple_of(p // 6 * FRT, FRT), FRT), cv_b, cu_b, p - 4)
+
+        @pl.when(lax.rem(i, 2) == 0)
+        def _():
+            for s in range(2):
                 p_copy(p, s).start()
+
+    @pl.loop(0, NF)
+    def _(n):
+        for r in range(XC):
+            at = slice(r * LANES, (r + 1) * LANES)
+            for k in range(2):
+                rest = slice(k * S, (k + 1) * S)
+                cut[n, at, rest] = cu_a[n, rest, at].T
+                cut[NF + n, at, rest] = cu_b[n, rest, at].T
 
     for n in (8, 9, 12, 13):
         p_in[n] = p_out[n]
@@ -362,24 +382,7 @@
         image_hop(da).wait_recv()
         return acc + d_in[1, 0, da].astype(F32)
 
-    @pl.loop(0, NF)
-    def _(i):
-        p = jnp.where(i < 2, i + 6, jnp.where(i < 4, i + 2, z_first(i - 4)))
-        w = jnp.where(i < 2, 1, 0)
-
-        @pl.when(i == 1)
-        def _():
-            for unit in (1, 3):
-                r_copy(unit).start()
-
-        @pl.when(i == 2)
-        def _():
-            spread(1)
-
-        @pl.when((i != 0) & (i != 2))
-        def _():
-            r_copy(back(p)).wait_recv()
-
+    def grid(p, w, cv, k):
         zs = []
         for s in range(2):
             re = r_in[2 * p + s, 0]
@@ -388,7 +391,32 @@
             bottom = jnp.concatenate([-im, -re], axis=1)
             both = jnp.concatenate([top, bottom], axis=0)
             zs.append(lax.dot_general(cut[2 * p + s], both, NN, preferred_element_type=F32).astype(BF16))
-        total[w] += lax.dot_general(jnp.concatenate(zs, axis=1), cv[p], NN, preferred_element_type=F32)
+        total[w] += lax.dot_general(jnp.concatenate(zs, axis=1), cv[k], NN, preferred_element_type=F32)
+
+    @pl.loop(0, 4)
+    def _(i):
+        p = jnp.where(i < 2, i + 6, i + 2)
+
+        @pl.when(i == 1)
+        def _():
+            for unit in (1, 3):
+                r_copy(unit).start()
+
+        @pl.when(i == 2)
+        def _():
+            spread(1)
+
+        @pl.when(lax.rem(i, 2) == 1)
+        def _():
+            r_copy(p).wait_recv()
+
+        grid(p, jnp.where(i < 2, 1, 0), cv_b, p - 4)
+
+    @pl.loop(0, 4)
+    def _(i):
+        p = z_first(i)
+        r_copy(back(p)).wait_recv()
+        grid(p, 0, cv_a, p)
 
     spread(0)
 
@@ -454,8 +482,10 @@
                 pltpu.VMEM((2 * NF, YC, LANES), F32),
                 pltpu.VMEM((2 * NF, 8, LANES), F32),
                 pltpu.VMEM((2 * NF, 8, LANES), F32),
-                pltpu.VMEM((NF, 4 * S, FW), BF16),
-                pltpu.VMEM((2 * NF, 2 * S, FRT), BF16),
+                pltpu.VMEM((4, 4 * S, FW), BF16),
+                pltpu.VMEM((4, 4 * S, FW), BF16),
+                pltpu.VMEM((NF, 2 * S, FRT), BF16),
+                pltpu.VMEM((NF, 2 * S, FRT), BF16),
                 pltpu.VMEM((2 * NF, FRT, 2 * S), BF16),
                 pltpu.VMEM((2 * NF, 2, S, S), BF16),
                 pltpu.VMEM((2 * NF, 2, S, S), BF16),

time: 61.7 us -> 56.9 us (0.922)
  Pallas kernels: 59.2 us -> 54.7 us
    pallas_call x1, Pallas kernels: 59.2 us -> 54.7 us  [body(): pl.pallas_call(kernel, name='major_cycle', out_shape=(pltpu.VMEM((ROWS, F...]
where the time goes in v5:
time: 56.9 us; the launch traced here: 56.8 us
  Pallas kernels  54.7 us (96%)
  local copies, waits for them, and re-layouts  1.45 us (3%)
  between operations  0.64 us (1%)
    pallas_call x1, Pallas kernels, body(): pl.pallas_call(kernel, name='major_cycle', out_shape=(pltpu.VMEM((ROWS, F...  54.7 us
    unnamed x2, local copies, waits for them, and re-layouts  1.45 us

profile of v5, /device:TPU:0, one launch (start us, length us, event | category | flops | bytes accessed | tf_op | source)
XLA Modules:
  0.0 56.8 jit_solution(10478364173669113157)
XLA Ops:
  0.6 54.7 %major_cycle.1 = (f32[16,2048]{1,0:T(8,128)S(1)}, bf16[8,2,128,128]{3,2,1,0:T(8,128)(2,1)S(1)}) custom-call(bf16[16,2048]{1,0:T(8,128)(2,1)} %model.1, bf16[8,2,128,128]{3,2,1,0:T(8,128)(2,1)} %observed.1, s32[8]{0:T(128)} %u_hbm.1, s32[8]{0:T(128)} %v_hbm.1, s32[2,8]{1,0:T(2,128)} %bitcast.1), custom_call_target="tpu_custom_call" | custom-call | tf_op jit(solution)/shard_map/major_cycle/pallas_call | solution.py:463
  55.4 0.7 %copy.9 = f32[16,2048]{1,0:T(8,128)} copy(f32[16,2048]{1,0:T(8,128)S(1)} %get-tuple-element.2) | data formatting | bytes 262144
  56.0 0.8 %copy.10 = bf16[8,2,128,128]{3,2,1,0:T(8,128)(2,1)} copy(bf16[8,2,128,128]{3,2,1,0:T(8,128)(2,1)S(1)} %get-tuple-element.3) | data formatting | bytes 1048576

commit v6 on v5

--- a/solution.py
+++ b/solution.py
@@ -261,6 +261,10 @@
         for s in range(2):
             tables(p, s, cv_a, cu_a, p)
 
+    for da in (0, 1, 3, 2):
+        model_hop(da).wait_recv()
+        ag_second(1, da)
+
     @pl.loop(0, 4)
     def _(p):
         for s in range(2):
@@ -271,12 +275,6 @@
     @pl.loop(0, 4)
     def _(i):
         p = z_first(i)
-
-        @pl.when(i == 1)
-        def _():
-            for da in (0, 1, 3, 2):
-                model_hop(da).wait_recv()
-                ag_second(1, da)
 
         predict(p, slice(0, FRT), cv_a, cu_a, p)
         for s in range(2):

time: 56.9 us -> 55.3 us (0.972)
  Pallas kernels: 54.7 us -> 53.1 us
    pallas_call x1, Pallas kernels: 54.7 us -> 53.1 us  [body(): pl.pallas_call(kernel, name='major_cycle', out_shape=(pltpu.VMEM((ROWS, F...]
where the time goes in v6:
time: 55.3 us; the launch traced here: 55.2 us
  Pallas kernels  53.1 us (96%)
  local copies, waits for them, and re-layouts  1.45 us (3%)
  between operations  0.64 us (1%)
    pallas_call x1, Pallas kernels, body(): pl.pallas_call(kernel, name='major_cycle', out_shape=(pltpu.VMEM((ROWS, F...  53.1 us
    unnamed x2, local copies, waits for them, and re-layouts  1.45 us

profile of v6, /device:TPU:0, one launch (start us, length us, event | category | flops | bytes accessed | tf_op | source)
XLA Modules:
  0.0 55.2 jit_solution(3133433681436849460)
XLA Ops:
  0.6 53.1 %major_cycle.1 = (f32[16,2048]{1,0:T(8,128)S(1)}, bf16[8,2,128,128]{3,2,1,0:T(8,128)(2,1)S(1)}) custom-call(bf16[16,2048]{1,0:T(8,128)(2,1)} %model.1, bf16[8,2,128,128]{3,2,1,0:T(8,128)(2,1)} %observed.1, s32[8]{0:T(128)} %u_hbm.1, s32[8]{0:T(128)} %v_hbm.1, s32[2,8]{1,0:T(2,128)} %bitcast.1), custom_call_target="tpu_custom_call" | custom-call | tf_op jit(solution)/shard_map/major_cycle/pallas_call | solution.py:461
  53.7 0.7 %copy.9 = f32[16,2048]{1,0:T(8,128)} copy(f32[16,2048]{1,0:T(8,128)S(1)} %get-tuple-element.2) | data formatting | bytes 262144
  54.4 0.8 %copy.10 = bf16[8,2,128,128]{3,2,1,0:T(8,128)(2,1)} copy(bf16[8,2,128,128]{3,2,1,0:T(8,128)(2,1)S(1)} %get-tuple-element.3) | data formatting | bytes 1048576

commit v7 on v6

--- a/solution.py
+++ b/solution.py
@@ -282,15 +282,15 @@
 
     @pl.loop(4, NF)
     def _(i):
-        p = z_first(i)
-
-        @pl.when(i == 6)
+        p = jnp.where(i == 4, 5, jnp.where(i == 5, 7, jnp.where(i == 6, 4, 6)))
+
+        @pl.when(i == 5)
         def _():
             ag_rest(1)
 
         predict(p, pl.ds(pl.multiple_of(p // 6 * FRT, FRT), FRT), cv_b, cu_b, p - 4)
 
-        @pl.when(lax.rem(i, 2) == 0)
+        @pl.when(i < 6)
         def _():
             for s in range(2):
                 p_copy(p, s).start()
@@ -338,7 +338,7 @@
         r_out[2 * p] = residual[lo]
         r_out[2 * p + 1] = residual[hi]
 
-        @pl.when((i < 2) | (i == 4) | (i == 6))
+        @pl.when((i != 5) & (i != 7))
         def _():
             r_copy(p).start()
 
@@ -394,11 +394,6 @@
     @pl.loop(0, 4)
     def _(i):
         p = jnp.where(i < 2, i + 6, i + 2)
-
-        @pl.when(i == 1)
-        def _():
-            for unit in (1, 3):
-                r_copy(unit).start()
 
         @pl.when(i == 2)
         def _():

time: 55.3 us -> 55.3 us (level)
  no operation moved by 1% of the time
where the time goes in v7:
time: 55.3 us; the launch traced here: 55.2 us
  Pallas kernels  53.1 us (96%)
  local copies, waits for them, and re-layouts  1.45 us (3%)
  between operations  0.64 us (1%)
    pallas_call x1, Pallas kernels, body(): pl.pallas_call(kernel, name='major_cycle', out_shape=(pltpu.VMEM((ROWS, F...  53.1 us
    unnamed x2, local copies, waits for them, and re-layouts  1.45 us

profile of v7, /device:TPU:0, one launch (start us, length us, event | category | flops | bytes accessed | tf_op | source)
XLA Modules:
  0.0 55.2 jit_solution(15674972117603489588)
XLA Ops:
  0.6 53.1 %major_cycle.1 = (f32[16,2048]{1,0:T(8,128)S(1)}, bf16[8,2,128,128]{3,2,1,0:T(8,128)(2,1)S(1)}) custom-call(bf16[16,2048]{1,0:T(8,128)(2,1)} %model.1, bf16[8,2,128,128]{3,2,1,0:T(8,128)(2,1)} %observed.1, s32[8]{0:T(128)} %u_hbm.1, s32[8]{0:T(128)} %v_hbm.1, s32[2,8]{1,0:T(2,128)} %bitcast.1), custom_call_target="tpu_custom_call" | custom-call | tf_op jit(solution)/shard_map/major_cycle/pallas_call | solution.py:456
  53.7 0.7 %copy.9 = f32[16,2048]{1,0:T(8,128)} copy(f32[16,2048]{1,0:T(8,128)S(1)} %get-tuple-element.2) | data formatting | bytes 262144
  54.4 0.8 %copy.10 = bf16[8,2,128,128]{3,2,1,0:T(8,128)(2,1)} copy(bf16[8,2,128,128]{3,2,1,0:T(8,128)(2,1)S(1)} %get-tuple-element.3) | data formatting | bytes 1048576
